TPU v7x, 128 devices: a whole 4x4x4 slice. The times are simulated.
128 devices in a mesh: row: 16 (over z, y), proto: 8 (over x, core).
Axes of the slice: x: 4, y: 4, z: 4, core: 2. Of those that a mesh axis runs over, the one named last changes fastest.
Arguments:
- embeddings: bfloat16 [4096, 256], P('row')
- queue_feats: bfloat16 [8192, 256], P('row')
- prototypes: bfloat16 [256, 65536], P('row', 'proto')
- crop_image: int32 [4096], P('row'), may hold values from 0 to 511, as said below
- fill_count: int32 [1], replicated, may hold values from 4096 to 8192
Outputs:
- grad_embed: float32 [4096, 256], P('row')
- grad_proto: float32 [256, 65536], P('row', 'proto')
- loss: float32 [1], replicated
Inputs may be any that keep to these rules, and one draw needn't show every extreme that they name: `crop_image`: each image index is named by exactly 8 crops, all within one aligned block of 256 rows (the rows of one device); block b holds images b * 32 to (b + 1) * 32 - 1.
All inputs are finite; a program needn't handle non-finite values.
Results may differ from a plain program's by a relative error of at most 0.002.
Values may be sent and summed in bfloat16 or wider, within the bound.
A program may use at most 64 MiB of HBM per device.

v0:
```python
import jax
import jax.numpy as jnp
from jax import lax
from jax.sharding import PartitionSpec as P

CROPS = 8
ITERS = 3


ENTROPY_SMOOTHER = 0.05
SOFTMAX_TEMPER = 0.1


def unit_rows(raw):
    values = raw.astype(jnp.float32)
    inverse = lax.rsqrt(jnp.sum(values * values, axis=1, keepdims=True) + 1e-06)
    return (values * inverse, inverse)


def body(embeddings, queue_feats, prototypes, crop_image, fill_count):
    normed_exact, inverse = unit_rows(embeddings)
    normed = normed_exact.astype(jnp.bfloat16)
    queue_normed = unit_rows(queue_feats)[0].astype(jnp.bfloat16)
    batch_rows = normed.shape[0]
    queue_rows = queue_normed.shape[0]
    feat_dim = normed.shape[1]
    image_local = batch_rows // CROPS
    local_image = crop_image - lax.axis_index("row") * image_local
    image_ids = jnp.arange(image_local, dtype=jnp.int32)
    membership = (image_ids[:, None] == local_image[None, :]).astype(jnp.bfloat16)
    gathered = lax.all_gather(prototypes, "row", axis=0, tiled=True)
    width_local = gathered.shape[1]
    block_cols = min(512, width_local)
    block_count = width_local // block_cols
    blocks = gathered.reshape(feat_dim, block_count, block_cols).transpose(1, 0, 2)
    offset = lax.axis_index("row") * queue_rows
    queue_live = (offset + jnp.arange(queue_rows, dtype=jnp.int32) < fill_count[0]).astype(
        jnp.float32
    )
    live = jnp.concatenate([jnp.ones((batch_rows,), jnp.float32), queue_live])
    rows_all = jnp.concatenate([normed, queue_normed], axis=0)

    def row_pass(column):

        def row_block(cumulative_accumulator, inputs_pair):
            proto_block, cluster_rescaling = inputs_pair
            centroid_similarity = jnp.dot(rows_all, proto_block, preferred_element_type=jnp.float32)
            return (
                cumulative_accumulator
                + jnp.sum(
                    jnp.exp(centroid_similarity / ENTROPY_SMOOTHER) * cluster_rescaling[None, :],
                    axis=1,
                ),
                None,
            )

        row_total, _ = lax.scan(
            row_block,
            jnp.zeros((rows_all.shape[0],), jnp.float32),
            (blocks, column.reshape(block_count, block_cols)),
        )
        return row_total

    centroid_matrix = live
    column = jnp.zeros((width_local,), jnp.float32)
    for sweep_index in range(ITERS):

        def column_block(proto_block):
            centroid_similarity = jnp.dot(rows_all, proto_block, preferred_element_type=jnp.float32)
            return jnp.sum(
                jnp.exp(centroid_similarity / ENTROPY_SMOOTHER) * centroid_matrix[:, None], axis=0
            )

        column = 1.0 / lax.psum(lax.map(column_block, blocks).reshape(width_local), "row")
        if sweep_index + 1 < ITERS:
            centroid_matrix = live / lax.psum(row_pass(column), "proto")
    column_blocks = column.reshape(block_count, block_cols)

    def totals(cumulative_accumulator, inputs_pair):
        proto_block, cluster_rescaling = inputs_pair
        centroid_similarity = jnp.dot(normed, proto_block, preferred_element_type=jnp.float32)
        allotment_share = jnp.sum(
            jnp.exp(centroid_similarity / ENTROPY_SMOOTHER) * cluster_rescaling[None, :], axis=1
        )
        softmax_portion = jnp.sum(jnp.exp(centroid_similarity / SOFTMAX_TEMPER), axis=1)
        return (
            (
                cumulative_accumulator[0] + allotment_share,
                cumulative_accumulator[1] + softmax_portion,
            ),
            None,
        )

    zeros_batch = jnp.zeros((batch_rows,), jnp.float32)
    (code_local, soft_local), _ = lax.scan(
        totals, (zeros_batch, zeros_batch), (blocks, column_blocks)
    )
    overall_mass_sum, softmax_total = lax.psum((code_local, soft_local), "proto")
    log_grand_total = jnp.log(softmax_total)
    member_weights = membership.astype(jnp.float32)

    def slopes(cumulative_accumulator, inputs_pair):
        proto_block, cluster_rescaling = inputs_pair
        centroid_similarity = jnp.dot(normed, proto_block, preferred_element_type=jnp.float32)
        cluster_allotment = (
            jnp.exp(centroid_similarity / ENTROPY_SMOOTHER)
            * cluster_rescaling[None, :]
            / overall_mass_sum[:, None]
        )
        per_image = jnp.dot(member_weights, cluster_allotment, precision=lax.Precision.HIGHEST)
        grouped = lax.dot_general(
            member_weights, per_image, (((0,), (0,)), ((), ())), precision=lax.Precision.HIGHEST
        )
        target_codes = (grouped - cluster_allotment) / (CROPS - 1)
        predicted_probs = jnp.exp(centroid_similarity / SOFTMAX_TEMPER) / softmax_total[:, None]
        logit_gradient = ((predicted_probs - target_codes) / SOFTMAX_TEMPER).astype(jnp.bfloat16)
        loss_portion = jnp.sum(
            target_codes * (log_grand_total[:, None] - centroid_similarity / SOFTMAX_TEMPER)
        )
        return (cumulative_accumulator + loss_portion, logit_gradient)

    loss_local, grad_blocks = lax.scan(slopes, jnp.zeros((), jnp.float32), (blocks, column_blocks))
    logit_gradient = grad_blocks.transpose(1, 0, 2).reshape(batch_rows, width_local)
    normed_local = lax.dot_general(
        logit_gradient, gathered, (((1,), (1,)), ((), ())), preferred_element_type=jnp.float32
    )
    normed_grad = lax.psum(normed_local, "proto")
    grad_proto = lax.psum_scatter(
        lax.dot_general(
            normed, logit_gradient, (((0,), (0,)), ((), ())), preferred_element_type=jnp.float32
        ),
        "row",
        scatter_dimension=0,
        tiled=True,
    )
    loss_total = lax.psum(loss_local, ("row", "proto"))
    loss = loss_total / (batch_rows * lax.axis_size("row"))
    grad_embed = inverse * (
        normed_grad - normed_exact * jnp.sum(normed_exact * normed_grad, axis=1, keepdims=True)
    )
    return (grad_embed, grad_proto, loss.reshape(1))


def solution(mesh):
    placed = (P("row", None), P("row", None), P("row", "proto"), P("row"), P())
    return jax.shard_map(
        body,
        mesh=mesh,
        in_specs=placed,
        out_specs=(P("row", None), P("row", "proto"), P()),
        check_vma=False,
    )
```

profile of v0, /device:TPU:1, one launch (start us, length us, event | category | flops | bytes accessed | tf_op | source)
XLA Modules:
  0.0 705.4 jit_solution(11963652205974593261)
XLA Ops:
  13.7 51.0 %all-gather.2.cloned.1.call-done = bf16[256,8192]{1,0:T(8,128)(2,1)} async-done(((bf16[16,8192]{1,0:T(8,128)(2,1)}), bf16[256,8192]{1,0:T(8,128)(2,1)}) %all-gather.2.cloned.1.call-update) | async-done | bytes 4194320 | tf_op jit(solution)/shard_map/all_gather | solution.py:31
  64.7 6.4 copy.16
  71.1 6.4 copy.23
  77.5 25.4 %while.78 = (s32[]{:T(128)}, f32[16,512]{1,0:T(8,128)S(1)}, bf16[16,256,512]{2,1,0:T(8,128)(2,1)}, bf16[768,256]{1,0:T(8,128)(2,1)S(1)}, f32[768]{0:T(1024)S(1)}, /*index=5*/s32[]{:T(128)}, s32[]{:T(128)}) while((s32[]{:T(128)}, f32[16,512]{1,0:T(8,128)S(1)}, bf16[16,256,512]{2,1,0:T(8,128)(2,1)}, bf16[768,256]{1,0:T(8,128)(2,1)S(1)}, ...), condition=%wide.region_4.5_spmd, body=%wide.region_2.4_spmd.sunk | while | flops 202505728 | bytes 664669 | solution.py:74
  103.0 58.3 %psum.63 = f32[8192]{0:T(1024)S(1)} all-reduce(f32[8192]{0:T(1024)S(1)} %bitcast.113), channel_id=1, replica_groups=mesh['row'=16,'proto'=8] {'row'}, use_global_device_ids=true, to_apply=%region_5.6 | all-reduce | flops 8192 | bytes 65536 | tf_op jit(solution)/shard_map/psum | solution.py:74
  161.3 24.7 %while.82 = (s32[]{:T(128)}, f32[768]{0:T(1024)S(1)}, bf16[16,256,512]{2,1,0:T(8,128)(2,1)}, bf16[768,256]{1,0:T(8,128)(2,1)S(1)}, f32[16,512]{1,0:T(8,128)S(1)}, /*index=5*/s32[]{:T(128)}, s32[]{:T(128)}) while((s32[]{:T(128)}, f32[768]{0:T(1024)S(1)}, bf16[16,256,512]{2,1,0:T(8,128)(2,1)}, bf16[768,256]{1,0:T(8,128)(2,1)S(1)}, ...), condition=%wide.region_8.9_spmd.clone, body=%wide.region_6.8_spmd.clone.sunk | while | flops 202507008 | bytes 673895 | solution.py:57
  185.9 26.8 %psum.64 = f32[768]{0:T(1024)S(1)} all-reduce(f32[768]{0:T(1024)S(1)} %get-tuple-element.225), channel_id=1, replica_groups=mesh['row'=16,'proto'=8] {'proto'}, use_global_device_ids=true, to_apply=%region_9.10 | all-reduce | flops 768 | bytes 6144 | tf_op jit(solution)/shard_map/psum | solution.py:76
  212.7 25.5 %while.79 = (s32[]{:T(128)}, f32[16,512]{1,0:T(8,128)S(1)}, bf16[16,256,512]{2,1,0:T(8,128)(2,1)}, bf16[768,256]{1,0:T(8,128)(2,1)S(1)}, f32[768]{0:T(1024)S(1)}, /*index=5*/s32[]{:T(128)}, s32[]{:T(128)}) while((s32[]{:T(128)}, f32[16,512]{1,0:T(8,128)S(1)}, bf16[16,256,512]{2,1,0:T(8,128)(2,1)}, bf16[768,256]{1,0:T(8,128)(2,1)S(1)}, ...), condition=%wide.region_12.13_spmd, body=%wide.region_10.12_spmd.sunk | while | flops 202505728 | bytes 664669 | solution.py:74
  212.7 1.5 multiply_reduce_fusion.14
  215.9 1.5 multiply_reduce_fusion.14
  238.2 56.3 %psum.65 = f32[8192]{0:T(1024)S(1)} all-reduce(f32[8192]{0:T(1024)S(1)} %bitcast.114), channel_id=1, replica_groups=mesh['row'=16,'proto'=8] {'row'}, use_global_device_ids=true, to_apply=%region_13.14 | all-reduce | flops 8192 | bytes 65536 | tf_op jit(solution)/shard_map/psum | solution.py:74
  294.5 24.7 %while.83 = (s32[]{:T(128)}, f32[768]{0:T(1024)S(1)}, bf16[16,256,512]{2,1,0:T(8,128)(2,1)}, bf16[768,256]{1,0:T(8,128)(2,1)S(1)}, f32[16,512]{1,0:T(8,128)S(1)}, /*index=5*/s32[]{:T(128)}, s32[]{:T(128)}) while((s32[]{:T(128)}, f32[768]{0:T(1024)S(1)}, bf16[16,256,512]{2,1,0:T(8,128)(2,1)}, bf16[768,256]{1,0:T(8,128)(2,1)S(1)}, ...), condition=%wide.region_16.17_spmd.clone, body=%wide.region_14.16_spmd.clone.sunk | while | flops 202507008 | bytes 673895 | solution.py:57
  319.2 25.7 %psum.66 = f32[768]{0:T(1024)S(1)} all-reduce(f32[768]{0:T(1024)S(1)} %get-tuple-element.227), channel_id=1, replica_groups=mesh['row'=16,'proto'=8] {'proto'}, use_global_device_ids=true, to_apply=%region_17.18 | all-reduce | flops 768 | bytes 6144 | tf_op jit(solution)/shard_map/psum | solution.py:76
  344.9 25.5 %while.80 = (s32[]{:T(128)}, f32[16,512]{1,0:T(8,128)S(1)}, bf16[16,256,512]{2,1,0:T(8,128)(2,1)}, bf16[768,256]{1,0:T(8,128)(2,1)S(1)}, f32[768]{0:T(1024)S(1)}, /*index=5*/s32[]{:T(128)}, s32[]{:T(128)}) while((s32[]{:T(128)}, f32[16,512]{1,0:T(8,128)S(1)}, bf16[16,256,512]{2,1,0:T(8,128)(2,1)}, bf16[768,256]{1,0:T(8,128)(2,1)S(1)}, ...), condition=%wide.region_20.21_spmd, body=%wide.region_18.20_spmd.sunk | while | flops 202505728 | bytes 664669 | solution.py:74
  348.1 1.5 multiply_reduce_fusion.15
  370.4 56.3 %psum.67 = f32[8192]{0:T(1024)S(1)} all-reduce(f32[8192]{0:T(1024)S(1)} %bitcast.115), channel_id=1, replica_groups=mesh['row'=16,'proto'=8] {'row'}, use_global_device_ids=true, to_apply=%region_21.22 | all-reduce | flops 8192 | bytes 65536 | tf_op jit(solution)/shard_map/psum | solution.py:74
  426.7 22.1 %while.84 = (s32[]{:T(128)}, f32[256]{0:T(256)S(1)}, f32[256]{0:T(256)S(1)}, bf16[16,256,512]{2,1,0:T(8,128)(2,1)}, bf16[256,256]{1,0:T(8,128)(2,1)S(1)}, /*index=5*/f32[16,512]{1,0:T(8,128)S(1)}, s32[]{:T(128)}, s32[]{:T(128)}) while((s32[]{:T(128)}, f32[256]{0:T(256)S(1)}, f32[256]{0:T(256)S(1)}, ...), condition=%wide.region_25.26_spmd.clone, body=%wide.region_22.25_spmd.clone.sunk | while | flops 67764736 | bytes 407663 | solution.py:95
  448.8 25.8 %all-reduce.1 = (f32[256]{0:T(256)S(1)}, f32[256]{0:T(256)S(1)}) all-reduce(f32[256]{0:T(256)S(1)} %get-tuple-element.229, f32[256]{0:T(256)S(1)} %get-tuple-element.230), channel_id=1, replica_groups=mesh['row'=16,'proto'=8] {'proto'}, use_global_device_ids=true, to_apply=%region_26.27 | all-reduce | flops 512 | bytes 4096 | tf_op jit(solution)/shard_map/psum | solution.py:98
  474.6 76.1 %while.81 = (s32[]{:T(128)}, f32[]{:T(128)}, bf16[16,256,512]{1,2,0:T(8,128)(2,1)}, bf16[16,256,512]{2,1,0:T(8,128)(2,1)}, bf16[256,256]{1,0:T(8,128)(2,1)S(1)},...) while((s32[]{:T(128)}, f32[]{:T(128)}, ...), condition=%wide.region_30.31_spmd.clone, body=%wide.region_28.30_spmd.clone.sunk | while | flops 170049536 | bytes 3946641 | solution.py:122
  550.7 5.5 fusion.45
  556.2 6.7 fusion.46
  563.0 62.9 %psum.71 = f32[]{:T(128)} all-reduce(f32[]{:T(128)} %get-tuple-element.232), channel_id=1, replica_groups=mesh['row'=16,'proto'=8] {'row','proto'}, use_global_device_ids=true, to_apply=%region_34.35 | all-reduce | flops 1 | bytes 8 | tf_op jit(solution)/shard_map/psum | solution.py:136
  627.7 1.8 fusion.41
  629.5 68.3 %reduce-scatter.2.cloned.1.call-done = f32[16,8192]{1,0:T(8,128)} async-done(((f32[256,8192]{1,0:T(8,128)}), f32[16,8192]{1,0:T(8,128)}) %reduce-scatter.2.cloned.1.call-update) | async-done | bytes 524304 | tf_op jit(solution)/shard_map/reduce_scatter | solution.py:128
  (357 shorter events, 212.9 us)
Async XLA Ops:
  7.2 57.5 %all-gather.2.cloned.1.call-start = ((), (), s32[]{:S(2)}) async-start(), calls=%async_computation.1 | async-start | bytes 4456448 | tf_op jit(solution)/shard_map/all_gather | solution.py:31
  7.9 618.6 %all-reduce.4.cloned.1.call-start = ((), (), s32[]{:S(2)}) async-start(), calls=%async_computation.2 | async-start | bytes 524288 | tf_op jit(solution)/shard_map/psum | solution.py:127
  556.2 141.6 %reduce-scatter.2.cloned.1.call-start = ((), (), s32[]{:S(2)}) async-start(), calls=%async_computation.3 | async-start | bytes 8912896 | tf_op jit(solution)/shard_map/reduce_scatter | solution.py:128
  563.0 63.6 %copy-start = (bf16[256,256]{1,0:T(8,128)(2,1)S(1)}, bf16[256,256]{1,0:T(8,128)(2,1)}, u32[]{:S(2)}) copy-start(bf16[256,256]{1,0:T(8,128)(2,1)} %param.19) | copy-start | bytes 393220
Sparse Core Ops, SparseCore 0:
  10.1 54.5 all-gather.1
  556.3 51.4 all-reduce.3
  611.8 85.9 reduce-scatter.1
where the time goes:
time: 711 us; the launch traced here: 705 us
  blocking collectives  312 us (44%)
  matrix products  205 us (29%)
  waiting for transfers between devices  120 us (17%)
  other arithmetic  21.7 us (3%)
  local copies, waits for them, and re-layouts  16.4 us (2%)
  between operations  16.4 us (2%)
  loops' own time  13.6 us (2%)
    psum x3, blocking collectives, body(): lax.psum(lax.map(column_block, blocks).reshape(width_local), 'row')  171 us
    dot_general x48, matrix products, column_block(): jnp.dot(rows_all, proto_block, preferred_element_type=jnp.float32)  72.5 us
    reduce_scatter x1, waiting for transfers between devices, body(): lax.psum_scatter(lax.dot_general(normed, logit_gradient, (((0,), (0,)), (...  68.3 us
    psum x1, blocking collectives, body(): loss_total = lax.psum(loss_local, ('row', 'proto'))  62.9 us
    psum x2, blocking collectives, body(): centroid_matrix = live / lax.psum(row_pass(column), 'proto')  52.5 us
    all_gather x1, waiting for transfers between devices, body(): gathered = lax.all_gather(prototypes, 'row', axis=0, tiled=True)  51 us
    dot_general x32, matrix products, row_block(): jnp.dot(rows_all, proto_block, preferred_element_type=jnp.float32)  47.4 us
    psum x1, blocking collectives, body(): lax.psum((code_local, soft_local), 'proto')  25.8 us
  transfers between devices with their start and end apart: 3, of which 2 were waited for; matrix products, arithmetic and copies ran while one was open for 2% of the time, Pallas kernels for 0%

commit v1 on v0

v1 whole, which is shorter than its diff:
```python
import functools
import math

import jax
import jax.numpy as jnp
from jax import lax
from jax.experimental import pallas as pl
from jax.experimental.pallas import tpu as pltpu
from jax.sharding import PartitionSpec as P

MESH = pl.DeviceIdType.MESH
F32 = jnp.float32
BF16 = jnp.bfloat16

CROPS = 8
ITERS = 3
SIDE = 4
LANES = 8
SCALE = 10.0 * math.log2(math.e)

B = 256
Q = 512
R = B + Q
D = 256
TILE = 256
NT = (((1,), (1,)), ((), ()))


def iota(shape, dim):
    return lax.broadcasted_iota(jnp.int32, shape, dim)


def split3(v):
    hi = v.astype(BF16).astype(F32)
    rest = v - hi
    mid = rest.astype(BF16).astype(F32)
    return hi, mid, rest - mid


def stack16(v):
    hi, mid, low = split3(v)
    rid = iota((16, v.shape[1]), 0)
    out = jnp.where(rid == 0, hi, jnp.where(rid == 1, mid, jnp.where(rid == 2, low, 0.0)))
    return out.astype(BF16)


def unit_rows(raw):
    values = raw.astype(F32)
    inverse = lax.rsqrt(jnp.sum(values * values, axis=1, keepdims=True) + 1e-06)
    return values * inverse, inverse


def kernel(
    fill_ref, emb_ref, queue_ref, proto_ref, image_ref,
    ge_ref, gp_ref, loss_ref,
    rows, protos, mass, score, grad, turned, soft_acc, row16, col16, colb,
    col_part, row_part, row_mid, col_in, rowx_in, rowy_in,
    row_soft, row_code, row_log,
    gp_out, gp_in, ng_out, ng_in, ng_all, lx_in, lz_in,
    a_send, a_recv, z_send, z_recv, r_send, r_recv,
    c_send, c_recv, x_send, x_recv, y_send, y_recv,
    g_send, g_recv, n_send, n_recv, h_send, h_recv, lx_send, lx_recv, lz_send, lz_recv,
):
    row = lax.axis_index("row")
    me = lax.axis_index("proto")
    z = row // SIDE
    y = lax.rem(row, SIDE)
    width = protos.shape[1]
    tiles = width // TILE

    def y_peer(d):
        return lax.rem(y + d, SIDE)

    def z_peer(d):
        return lax.rem(z + d, SIDE)

    def p_peer(d):
        return lax.rem(me + d, LANES)

    def remote(src, dst, send, recv, device):
        copy = pltpu.make_async_remote_copy(
            src_ref=src, dst_ref=dst, send_sem=send, recv_sem=recv,
            device_id=device, device_id_type=MESH,
        )
        copy.start()
        return copy

    barrier = pltpu.get_barrier_semaphore()
    count = 0
    for dz in range(SIDE):
        for dy in range(SIDE):
            if dz or dy:
                pl.semaphore_signal(
                    barrier, inc=1, device_id=(z_peer(dz) * SIDE + y_peer(dy), me), device_id_type=MESH
                )
                count += 1
    for dy in range(SIDE):
        for dp in range(1, LANES):
            pl.semaphore_signal(
                barrier, inc=1, device_id=(z * SIDE + y_peer(dy), p_peer(dp)), device_id_type=MESH
            )
            count += 1

    image = image_ref[...].astype(F32)
    wide = jnp.broadcast_to(image, (B, B))
    rid, cid = iota((B, B), 0), iota((B, B), 1)
    tall = jnp.sum(jnp.where(rid == cid, wide, 0.0), axis=1, keepdims=True)
    same = jnp.where(wide == tall, 1.0, 0.0)
    base = (row * (B // CROPS)).astype(F32)
    place = jnp.sum(jnp.where(rid < cid, same, 0.0), axis=0, keepdims=True) * (B // CROPS) + (image - base)
    forward = jnp.where(rid.astype(F32) == place, 1.0, 0.0).astype(BF16)
    exact, _ = unit_rows(emb_ref[...])
    ordered = jnp.dot(forward, exact.astype(BF16), preferred_element_type=F32).astype(BF16)
    rows[y, 0:B, :] = ordered
    rows[y, B:R, :] = unit_rows(queue_ref[...])[0].astype(BF16)
    dims = pl.ds(pl.multiple_of(row * 16, 16), 16)
    protos[dims, :] = proto_ref[:, pl.ds(pl.multiple_of(y * width, width), width)]

    pl.semaphore_wait(barrier, count)

    first = []
    for d in (1, 3, 2):
        first.append(
            remote(
                proto_ref.at[:, pl.ds(pl.multiple_of(y_peer(d) * width, width), width)],
                protos.at[dims, :], a_send.at[d], a_recv.at[d], (z * SIDE + y_peer(d), me),
            )
        )
    row_copies = {}
    for d in (1, 3, 2):
        row_copies[d] = remote(
            rows.at[y], rows.at[y], r_send.at[d], r_recv.at[d], (z * SIDE + y_peer(d), me)
        )
    for copy in first:
        copy.wait()
    second = []
    plane = pl.ds(pl.multiple_of(z * 64, 64), 64)
    for d in (1, 3, 2):
        second.append(
            remote(
                protos.at[plane, :], protos.at[plane, :], z_send.at[d], z_recv.at[d],
                (z_peer(d) * SIDE + y, me),
            )
        )
    soft_acc[...] = jnp.zeros_like(soft_acc)
    col_part[...] = jnp.zeros_like(col_part)
    fill = fill_ref[0]
    for copy in second:
        copy.wait()

    for d in (0, 1, 3, 2):
        if d:
            row_copies[d].wait()
        slot = lax.rem(y + SIDE - d, SIDE)
        lane = iota((16, R), 1)
        first_queue = (z * SIDE + slot) * Q - B
        alive = jnp.logical_or(lane < B, lane + first_queue < fill)
        live16 = jnp.where(jnp.logical_and(alive, iota((16, R), 0) == 0), 1.0, 0.0).astype(BF16)

        def score_tile(j, carry, slot=slot, live16=live16):
            cols = pl.ds(pl.multiple_of(j * TILE, TILE), TILE)
            total = jnp.dot(rows[slot], protos[:, cols], preferred_element_type=F32)
            crop = total[0:B]
            score[slot, :, cols] = crop
            soft = jnp.exp2(crop * SCALE)
            soft_acc[slot] += soft[:, 0:128] + soft[:, 128:256]
            mass[slot, 0:B, cols] = (soft * soft).astype(BF16)
            mass[slot, B:R, cols] = jnp.exp2(total[B:R] * (2.0 * SCALE)).astype(BF16)
            part = jnp.dot(live16, mass[slot, :, cols], preferred_element_type=F32)
            col_part[0, pl.ds(j, 1), :] += part[0:1, :]
            return carry

        lax.fori_loop(0, tiles, score_tile, 0)

    def column_exchange(t):
        copies = []
        for d in (2, 1, 3):
            copies.append(
                remote(
                    col_part.at[t], col_in.at[t, z], c_send.at[t, d], c_recv.at[t, d],
                    (z_peer(d) * SIDE + y, me),
                )
            )
        col_in[t, z] = col_part[t]
        for copy in copies:
            copy.wait()
        column = 1.0 / (col_in[t, 0] + col_in[t, 1] + col_in[t, 2] + col_in[t, 3])
        for j in range(tiles):
            col16[:, j * TILE:(j + 1) * TILE] = stack16(column[j:j + 1, :])
            if t == ITERS - 1:
                colb[:, j * TILE:(j + 1) * TILE] = jnp.broadcast_to(column[j:j + 1, :], (8, TILE))

    def row_exchange(t):
        copies = []
        for d in (4, 3, 5, 2, 6, 1, 7):
            copies.append(
                remote(
                    row_part.at[t], rowx_in.at[t, me], x_send.at[t, d], x_recv.at[t, d],
                    (row, p_peer(d)),
                )
            )
        rowx_in[t, me] = row_part[t]
        for copy in copies:
            copy.wait()
        total = rowx_in[t, 0]
        for k in range(1, LANES):
            total = total + rowx_in[t, k]
        row_mid[t] = total
        copies = []
        for d in (2, 1, 3):
            copies.append(
                remote(
                    row_mid.at[t], rowy_in.at[t, y], y_send.at[t, d], y_recv.at[t, d],
                    (z * SIDE + y_peer(d), me),
                )
            )
        rowy_in[t, y] = total
        for copy in copies:
            copy.wait()
        return rowy_in[t, 0] + rowy_in[t, 1] + rowy_in[t, 2] + rowy_in[t, 3]

    half = R // 2
    rid8, lane8 = iota((8, half), 0), iota((8, half), 1)
    spot = lax.rem(rid8, 2) * half + lane8
    queue_row = (z * SIDE + rid8 // 2) * Q + spot - B
    live = jnp.where(jnp.logical_or(spot < B, queue_row < fill), 1.0, 0.0)

    for t in range(ITERS):
        column_exchange(t)
        if t + 1 == ITERS:
            break

        for slot in range(SIDE):
            part = lax.dot_general(col16[...], mass[slot], NT, preferred_element_type=F32)
            part = jnp.sum(part, axis=0, keepdims=True)
            row_part[t, 2 * slot:2 * slot + 1, :] = part[:, 0:half]
            row_part[t, 2 * slot + 1:2 * slot + 2, :] = part[:, half:R]
        weight = live / row_exchange(t)
        for slot in range(SIDE):
            vector = jnp.concatenate(
                [weight[2 * slot:2 * slot + 1, :], weight[2 * slot + 1:2 * slot + 2, :]], axis=1
            )
            row16[slot] = stack16(vector)

        def column_tile(j, carry, t=t):
            cols = pl.ds(pl.multiple_of(j * TILE, TILE), TILE)
            part = jnp.dot(row16[0], mass[0, :, cols], preferred_element_type=F32)
            for slot in range(1, SIDE):
                part = part + jnp.dot(row16[slot], mass[slot, :, cols], preferred_element_type=F32)
            col_part[t + 1, pl.ds(j, 1), :] = jnp.sum(part, axis=0, keepdims=True)
            return carry

        lax.fori_loop(0, tiles, column_tile, 0)

    last = ITERS - 1
    for slot in range(SIDE):
        part = lax.dot_general(col16[...], mass[slot, 0:B, :], NT, preferred_element_type=F32)
        row_part[last, 2 * slot:2 * slot + 1, 0:B] = jnp.sum(part, axis=0, keepdims=True)
        row_part[last, 2 * slot + 1:2 * slot + 2, 0:B] = jnp.concatenate(
            [
                jnp.sum(soft_acc[slot, 0:128, :].T, axis=0, keepdims=True),
                jnp.sum(soft_acc[slot, 128:256, :].T, axis=0, keepdims=True),
            ],
            axis=1,
        )
        row_part[last, 2 * slot:2 * slot + 2, B:half] = jnp.ones((2, half - B), F32)
        eye = jnp.where(rid == cid, 1.0, 0.0).astype(BF16)
        turned[:, slot * B:(slot + 1) * B] = lax.dot_general(
            eye, rows[slot, 0:B, :], NT, preferred_element_type=F32
        ).astype(BF16)
    sums = row_exchange(last)
    for slot in range(SIDE):
        code = sums[2 * slot:2 * slot + 1, 0:B]
        soft = sums[2 * slot + 1:2 * slot + 2, 0:B]
        for target, value in (
            (row_code, (10.0 / (CROPS - 1)) / code),
            (row_soft, 10.0 / soft),
            (row_log, 0.1 * jnp.log(soft)),
        ):
            for h in range(2):
                target[slot, h * 128:(h + 1) * 128, :] = jnp.broadcast_to(
                    value[:, h * 128:(h + 1) * 128], (128, 128)
                ).T

    images = B // CROPS

    def slope_tile(j, lost):
        cols = pl.ds(pl.multiple_of(j * TILE, TILE), TILE)
        for slot in range(SIDE):
            for h in range(TILE // 128):
                lanes = pl.ds(pl.multiple_of(j * TILE + h * 128, 128), 128)
                column = colb[:, lanes]
                for i in range(images // 8):
                    softs, parts, scores = [], [], []
                    for c in range(CROPS):
                        at = slice(c * images + i * 8, c * images + i * 8 + 8)
                        s = score[slot, at, lanes]
                        e = jnp.exp2(s * SCALE)
                        parts.append(e * e * column * row_code[slot, at, :])
                        softs.append(e * row_soft[slot, at, :])
                        scores.append(row_log[slot, at, :] - s)
                    total = parts[0]
                    for c in range(1, CROPS):
                        total = total + parts[c]
                    for c in range(0, CROPS):
                        at = slice(slot * B + c * images + i * 8, slot * B + c * images + i * 8 + 8)
                        goal = total - parts[c]
                        lost = lost + goal * scores[c]
                        grad[at, lanes] = (softs[c] - goal).astype(BF16)
        gp_out[:, cols] = jnp.dot(turned[...], grad[:, cols], preferred_element_type=F32).astype(BF16)
        return lost

    lost = jnp.zeros((8, 128), F32)
    gp_copies = []
    halves = gp_out.shape[1] // gp_in.shape[-1]
    span = width // halves
    for h in range(halves):
        lost = lax.fori_loop(h * tiles // halves, (h + 1) * tiles // halves, slope_tile, lost)
        n = 0
        for dz, dy in (
            (2, 2), (2, 1), (2, 3), (1, 2), (3, 2), (1, 1), (1, 3), (3, 1), (3, 3),
            (2, 0), (0, 2), (1, 0), (3, 0), (0, 1), (0, 3),
        ):
            peer = z_peer(dz) * SIDE + y_peer(dy)
            gp_copies.append(
                remote(
                    gp_out.at[pl.ds(pl.multiple_of(peer * 16, 16), 16), h * span:(h + 1) * span],
                    gp_in.at[z, y, h], g_send.at[h, n], g_recv.at[h, n], (peer, me),
                )
            )
            n += 1

    lx_in[me] = lost
    loss_copies = []
    for d in range(1, LANES):
        loss_copies.append(
            remote(lx_in.at[me], lx_in.at[me], lx_send.at[d], lx_recv.at[d], (row, p_peer(d)))
        )

    def normed_block(slot, carry):
        block = pl.ds(pl.multiple_of(slot * B, B), B)
        ng_out[slot] = lax.dot_general(grad[block, :], protos[...], NT, preferred_element_type=F32)
        return carry

    lax.fori_loop(0, SIDE, normed_block, 0)
    slab = B // LANES
    ng_copies = []
    n = 0
    for dy in (2, 1, 3, 0):
        for dp in (4, 3, 5, 2, 6, 1, 7, 0):
            if dy == 0 and dp == 0:
                continue
            to_y, to_p = y_peer(dy), p_peer(dp)
            ng_copies.append(
                remote(
                    ng_out.at[to_y, pl.ds(pl.multiple_of(to_p * slab, slab), slab), :],
                    ng_in.at[y * LANES + me], n_send.at[n], n_recv.at[n], (z * SIDE + to_y, to_p),
                )
            )
            n += 1
    ng_in[y * LANES + me] = ng_out[y, pl.ds(pl.multiple_of(me * slab, slab), slab), :]
    for copy in loss_copies:
        copy.wait()
    lost = lx_in[0]
    for k in range(1, LANES):
        lost = lost + lx_in[k]
    lz_in[row] = lost
    loss_copies = []
    n = 0
    for dz in range(SIDE):
        for dy in range(SIDE):
            if dz or dy:
                loss_copies.append(
                    remote(
                        lz_in.at[row], lz_in.at[row], lz_send.at[n], lz_recv.at[n],
                        (z_peer(dz) * SIDE + y_peer(dy), me),
                    )
                )
                n += 1
    for copy in ng_copies:
        copy.wait()
    total = ng_in[0]
    for k in range(1, SIDE * LANES):
        total = total + ng_in[k]
    ng_all[me] = total
    all_copies = []
    for d in (4, 3, 5, 2, 6, 1, 7):
        all_copies.append(
            remote(ng_all.at[me], ng_all.at[me], h_send.at[d], h_recv.at[d], (row, p_peer(d)))
        )

    for copy in loss_copies:
        copy.wait()
    lost = lz_in[0]
    for k in range(1, SIDE * SIDE):
        lost = lost + lz_in[k]
    loss_ref[0] = jnp.sum(lost) * (1.0 / (B * SIDE * SIDE))

    for h in range(halves):
        gp_in[z, y, h] = gp_out[dims, h * span:(h + 1) * span]
    for copy in gp_copies:
        copy.wait()
    for k in range(SIDE):
        for h in range(halves):
            start = k * width + h * span
            gp_ref[:, start:start + span] = (
                gp_in[0, k, h].astype(F32) + gp_in[1, k, h].astype(F32)
                + gp_in[2, k, h].astype(F32) + gp_in[3, k, h].astype(F32)
            )

    for copy in all_copies:
        copy.wait()
    wide = jnp.broadcast_to(image_ref[...].astype(F32), (B, B))
    rid, cid = iota((B, B), 0), iota((B, B), 1)
    tall = jnp.sum(jnp.where(rid == cid, wide, 0.0), axis=1, keepdims=True)
    same = jnp.where(wide == tall, 1.0, 0.0)
    place = jnp.sum(jnp.where(cid < rid, same, 0.0), axis=1, keepdims=True) * (B // CROPS) + (tall - base)
    back = jnp.where(cid.astype(F32) == place, 1.0, 0.0).astype(BF16)
    gathered = ng_all[...].reshape(B, D)
    normed_grad = jnp.zeros((B, D), F32)
    for term in split3(gathered):
        normed_grad = normed_grad + jnp.dot(back, term.astype(BF16), preferred_element_type=F32)
    exact, inverse = unit_rows(emb_ref[...])
    along = jnp.sum(exact * normed_grad, axis=1, keepdims=True)
    ge_ref[...] = inverse * (normed_grad - exact * along)


def body(embeddings, queue_feats, prototypes, crop_image, fill_count):
    width = prototypes.shape[1] // SIDE
    half = R // 2
    halves = 2
    vmem = pl.BlockSpec(memory_space=pltpu.VMEM)
    smem = pl.BlockSpec(memory_space=pltpu.SMEM)
    dma = pltpu.SemaphoreType.DMA
    slab = B // LANES
    scratch = [
        pltpu.VMEM((SIDE, R, D), BF16),
        pltpu.VMEM((D, width), BF16),
        pltpu.VMEM((SIDE, R, width), BF16),
        pltpu.VMEM((SIDE, B, width), F32),
        pltpu.VMEM((SIDE * B, width), BF16),
        pltpu.VMEM((D, SIDE * B), BF16),
        pltpu.VMEM((SIDE, B, 128), F32),
        pltpu.VMEM((SIDE, 16, R), BF16),
        pltpu.VMEM((16, width), BF16),
        pltpu.VMEM((8, width), F32),
        pltpu.VMEM((ITERS, 8, width // 8), F32),
        pltpu.VMEM((ITERS, 8, half), F32),
        pltpu.VMEM((ITERS, 8, half), F32),
        pltpu.VMEM((ITERS, SIDE, 8, width // 8), F32),
        pltpu.VMEM((ITERS, LANES, 8, half), F32),
        pltpu.VMEM((ITERS, SIDE, 8, half), F32),
        pltpu.VMEM((SIDE, B, 128), F32),
        pltpu.VMEM((SIDE, B, 128), F32),
        pltpu.VMEM((SIDE, B, 128), F32),
        pltpu.VMEM((D, width), BF16),
        pltpu.VMEM((SIDE, SIDE, halves, 16, width // halves), BF16),
        pltpu.VMEM((SIDE, B, D), F32),
        pltpu.VMEM((SIDE * LANES, slab, D), F32),
        pltpu.VMEM((LANES, slab, D), F32),
        pltpu.VMEM((LANES, 8, 128), F32),
        pltpu.VMEM((SIDE * SIDE, 8, 128), F32),
        dma((SIDE,)), dma((SIDE,)), dma((SIDE,)), dma((SIDE,)), dma((SIDE,)), dma((SIDE,)),
        dma((ITERS, SIDE)), dma((ITERS, SIDE)), dma((ITERS, LANES)), dma((ITERS, LANES)),
        dma((ITERS, SIDE)), dma((ITERS, SIDE)),
        dma((halves, 15)), dma((halves, 15)), dma((31,)), dma((31,)), dma((LANES,)), dma((LANES,)),
        dma((LANES,)), dma((LANES,)), dma((15,)), dma((15,)),
    ]
    return pl.pallas_call(
        kernel,
        name="swav",
        out_shape=(
            jax.ShapeDtypeStruct((B, D), F32),
            jax.ShapeDtypeStruct((prototypes.shape[0], prototypes.shape[1]), F32),
            jax.ShapeDtypeStruct((1,), F32),
        ),
        in_specs=[smem, vmem, vmem, vmem, vmem],
        out_specs=(vmem, vmem, smem),
        scratch_shapes=scratch,
        compiler_params=pltpu.CompilerParams(
            collective_id=0, has_side_effects=True, vmem_limit_bytes=60 * 1024 * 1024
        ),
    )(fill_count, embeddings, queue_feats, prototypes, crop_image.reshape(1, B))


def solution(mesh):
    placed = (P("row", None), P("row", None), P("row", "proto"), P("row"), P())
    return jax.shard_map(
        body,
        mesh=mesh,
        in_specs=placed,
        out_specs=(P("row", None), P("row", "proto"), P()),
        check_vma=False,
    )
```

time: 711 us -> 131 us (0.18)
  blocking collectives: 312 us -> 0 us
  matrix products: 205 us -> 0 us
  Pallas kernels: 0 us -> 125 us
  waiting for transfers between devices: 120 us -> 0 us
  other arithmetic: 21.7 us -> 0 us
  local copies, waits for them, and re-layouts: 16.4 us -> 2.52 us
  loops' own time: 13.6 us -> 0 us
  between operations: 16.4 us -> 3.06 us
    psum x7 -> x0, blocking collectives: 312 us -> none  [the longest x3 171 us: body(): lax.psum(lax.map(column_block, blocks).reshape(width_local), 'row')]
    dot_general x146 -> x0, matrix products: 205 us -> none  [the longest x48 72.5 us: column_block(): jnp.dot(rows_all, proto_block, preferred_element_type=jnp.float32)]
    pallas_call x0 -> x1, Pallas kernels: none -> 125 us  [body(): pl.pallas_call(kernel, name='swav', out_shape=(jax.ShapeDtypeStruct((B, D...]
    reduce_scatter x1 -> x0, waiting for transfers between devices: 68.3 us -> none  [body(): lax.psum_scatter(lax.dot_general(normed, logit_gradient, (((0,), (0,)), (...]
    all_gather x1 -> x0, waiting for transfers between devices: 51 us -> none  [body(): gathered = lax.all_gather(prototypes, 'row', axis=0, tiled=True)]
    another operation x7 -> x0, loops' own time: 13.6 us -> none  [the longest x1 10.7 us: body(): lax.scan(slopes, jnp.zeros((), jnp.float32), (blocks, column_blocks))]
    dynamic_update_slice x16 -> x0, other arithmetic: 13.3 us -> none  [body(): lax.scan(slopes, jnp.zeros((), jnp.float32), (blocks, column_blocks))]
  transfers between devices with their start and end apart: 3 -> 0, of which waited for: 2 -> 0; matrix products, arithmetic and copies ran while one was open for 2% -> 0% of each run, Pallas kernels for 0% -> 0%
where the time goes in v1:
time: 131 us
  Pallas kernels  125 us (95%)
  between operations  3.06 us (2%)
  local copies, waits for them, and re-layouts  2.52 us (2%)
    pallas_call x1, Pallas kernels, body(): pl.pallas_call(kernel, name='swav', out_shape=(jax.ShapeDtypeStruct((B, D...  125 us

profile of v1, /device:TPU:1, one launch (start us, length us, event | category | flops | bytes accessed | tf_op | source)
XLA Modules:
  0.0 130.6 jit_solution(9615848096712018790)
XLA Ops:
  1.3 125.0 %swav.1 = (f32[256,256]{1,0:T(8,128)}, f32[16,8192]{1,0:T(8,128)}, f32[1]{0:T(128)}) custom-call(s32[1]{0:T(128)S(6)} %copy.11.fill_ref, bf16[256,256]{1,0:T(8,128)(2,1)} %emb_ref.1, bf16[512,256]{1,0:T(8,128)(2,1)} %queue_ref.1, bf16[16,8192]{1,0:T(8,128)(2,1)} %proto_ref.1, s32[1,256]{1,0:T(1,128)} %bitcast.1), custom_call_target="tpu_custom_call" | custom-call | tf_op jit(solution)/shard_map/swav/pallas_call | solution.py:469
  126.3 0.0 copy-start
  126.3 1.7 %copy.12 = f32[256,256]{1,0:T(8,128)} copy(f32[256,256]{1,0:T(8,128)} %get-tuple-element.6) | data formatting | bytes 524288
  128.0 0.0 copy-done
  128.0 0.8 copy.13
Async XLA Ops:
  126.3 1.7 %copy-start = (f32[16,8192]{1,0:T(8,128)S(1)}, f32[16,8192]{1,0:T(8,128)}, u32[]{:S(2)}) copy-start(f32[16,8192]{1,0:T(8,128)} %get-tuple-element.7) | copy-start | bytes 1572868

commit v2 on v1

v2 whole, which is shorter than its diff:
```python
import functools
import math

import jax
import jax.numpy as jnp
from jax import lax
from jax.experimental import pallas as pl
from jax.experimental.pallas import tpu as pltpu
from jax.sharding import PartitionSpec as P

MESH = pl.DeviceIdType.MESH
F32 = jnp.float32
BF16 = jnp.bfloat16

CROPS = 8
ITERS = 3
SIDE = 4
LANES = 8
SCALE = 10.0 * math.log2(math.e)

B = 256
Q = 512
R = B + Q
D = 256
TILE = 256
NT = (((1,), (1,)), ((), ()))


def iota(shape, dim):
    return lax.broadcasted_iota(jnp.int32, shape, dim)


def split3(v):
    hi = v.astype(BF16).astype(F32)
    rest = v - hi
    mid = rest.astype(BF16).astype(F32)
    return hi, mid, rest - mid


def stack16(v):
    hi, mid, low = split3(v)
    rid = iota((16, v.shape[1]), 0)
    out = jnp.where(rid == 0, hi, jnp.where(rid == 1, mid, jnp.where(rid == 2, low, 0.0)))
    return out.astype(BF16)


def unit_rows(raw):
    values = raw.astype(F32)
    inverse = lax.rsqrt(jnp.sum(values * values, axis=1, keepdims=True) + 1e-06)
    return values * inverse, inverse


def kernel(
    fill_ref, emb_ref, queue_ref, proto_ref, image_ref,
    ge_ref, gp_ref, loss_ref,
    rows, protos, mass, score, grad, turned, soft_acc, col_acc, alive, row16, col16, colb,
    col_part, row_part, row_pair, row_mid, col_in, rowc_in, rowx_in, rowy_in,
    row_soft, row_code, unit, factor, back,
    gp_out, gp_in, ng_out, ng_in, ng_sum, ngy_in, ng_all, lx_in, lz_in,
    a_send, a_recv, z_send, z_recv, r_send, r_recv, f_send, f_recv,
    c_send, c_recv, s_send, s_recv, x_send, x_recv, y_send, y_recv,
    g_send, g_recv, n_send, n_recv, m_send, m_recv, h_send, h_recv, lx_send, lx_recv, lz_send, lz_recv,
):
    row = lax.axis_index("row")
    me = lax.axis_index("proto")
    z = row // SIDE
    y = lax.rem(row, SIDE)
    core = lax.rem(me, 2)
    chip = me // 2
    sibling = chip * 2 + (1 - core)
    width = protos.shape[1]
    tiles = width // TILE
    chunks = gp_in.shape[2]
    span = width // chunks

    def y_peer(d):
        return lax.rem(y + d, SIDE)

    def z_peer(d):
        return lax.rem(z + d, SIDE)

    def p_peer(d):
        return lax.rem(me + d, LANES)

    def remote(src, dst, send, recv, device):
        copy = pltpu.make_async_remote_copy(
            src_ref=src, dst_ref=dst, send_sem=send, recv_sem=recv,
            device_id=device, device_id_type=MESH,
        )
        copy.start()
        return copy

    barrier = pltpu.get_barrier_semaphore()
    count = 0
    for dz in range(SIDE):
        for dy in range(SIDE):
            if dz or dy:
                pl.semaphore_signal(
                    barrier, inc=1, device_id=(z_peer(dz) * SIDE + y_peer(dy), me), device_id_type=MESH
                )
                count += 1
    for dp in range(1, LANES):
        pl.semaphore_signal(barrier, inc=1, device_id=(row, p_peer(dp)), device_id_type=MESH)
        count += 1
    for dy in range(1, SIDE):
        pl.semaphore_signal(
            barrier, inc=1, device_id=(z * SIDE + y_peer(dy), sibling), device_id_type=MESH
        )
        count += 1

    image = image_ref[...].astype(F32)
    wide = jnp.broadcast_to(image, (B, B))
    rid, cid = iota((B, B), 0), iota((B, B), 1)
    tall = jnp.sum(jnp.where(rid == cid, wide, 0.0), axis=1, keepdims=True)
    same = jnp.where(wide == tall, 1.0, 0.0)
    base = (row * (B // CROPS)).astype(F32)
    place = jnp.sum(jnp.where(rid < cid, same, 0.0), axis=0, keepdims=True) * (B // CROPS) + (image - base)
    forward = jnp.where(rid.astype(F32) == place, 1.0, 0.0).astype(BF16)
    exact, _ = unit_rows(emb_ref[...])
    ordered = jnp.dot(forward, exact.astype(BF16), preferred_element_type=F32).astype(BF16)
    rows[y, 0:B, :] = ordered
    rows[y, B:R, :] = unit_rows(queue_ref[...])[0].astype(BF16)
    dims = pl.ds(pl.multiple_of(row * 16, 16), 16)
    protos[dims, :] = proto_ref[:, pl.ds(pl.multiple_of(y * width, width), width)]

    pl.semaphore_wait(barrier, count)

    first = {}
    for k in range(chunks):
        for d in (1, 3, 2):
            first[k, d] = remote(
                proto_ref.at[:, pl.ds(pl.multiple_of(y_peer(d) * width + k * span, span), span)],
                protos.at[dims, k * span:(k + 1) * span], a_send.at[k, d], a_recv.at[k, d],
                (z * SIDE + y_peer(d), me),
            )
    shared = pl.ds(pl.multiple_of(core * (R // 2), R // 2), R // 2)
    row_copies = {}
    for d in (1, 3, 2):
        row_copies[d] = remote(
            rows.at[y, shared, :], rows.at[y, shared, :], r_send.at[d], r_recv.at[d],
            (z * SIDE + y_peer(d), me),
        )
    second = {}
    plane = pl.ds(pl.multiple_of(z * 64, 64), 64)
    for k in range(chunks):
        for d in (1, 3, 2):
            first[k, d].wait()
        for d in (1, 3, 2):
            part = protos.at[plane, k * span:(k + 1) * span]
            second[k, d] = remote(
                part, part, z_send.at[k, d], z_recv.at[k, d], (z_peer(d) * SIDE + y, me)
            )

    soft_acc[...] = jnp.zeros_like(soft_acc)
    col_acc[...] = jnp.zeros_like(col_acc)
    fill = fill_ref[0]
    for slot in range(SIDE):
        place = (z * SIDE + slot) * Q + iota((Q, 128), 0)
        alive[slot] = jnp.where(place < fill, 1.0, 0.0)
    place = jnp.sum(jnp.where(cid < rid, same, 0.0), axis=1, keepdims=True) * (B // CROPS) + (tall - base)
    back[...] = jnp.where(cid.astype(F32) == place, 1.0, 0.0).astype(BF16)
    exact, inverse = unit_rows(emb_ref[...])
    unit[...] = exact
    factor[...] = jnp.broadcast_to(inverse, (B, 128))

    def score_chunk(slot, k):
        for h in range(span // TILE):
            cols = pl.ds(pl.multiple_of(k * span + h * TILE, TILE), TILE)
            total = jnp.dot(rows[slot], protos[:, cols], preferred_element_type=F32)
            crop = total[0:B] * SCALE
            score[slot, :, cols] = crop
            soft = jnp.exp2(crop)
            soft_acc[slot] += soft[:, 0:128] + soft[:, 128:256]
            code = soft * soft
            mass[slot, 0:B, cols] = code.astype(BF16)
            rest = jnp.exp2(total[B:R] * (2.0 * SCALE))
            mass[slot, B:R, cols] = rest.astype(BF16)
            live = alive[slot]
            for g in range(TILE // 128):
                lanes = slice(g * 128, (g + 1) * 128)
                part = jnp.sum(code[:, lanes].reshape(B // 8, 8, 128), axis=0)
                part = part + jnp.sum((rest[:, lanes] * live).reshape(Q // 8, 8, 128), axis=0)
                at = pl.ds(pl.multiple_of(k * span + h * TILE + g * 128, 128), 128)
                col_acc[:, at] += part

    def score_many(first_slot, slots, first_chunk, many):
        def step(i, carry):
            n = first_slot + i // many
            score_chunk(lax.rem(y + n + n // 2, SIDE), first_chunk + lax.rem(i, many))
            return carry

        lax.fori_loop(0, slots * many, step, 0)

    def z_arrived(k):
        for d in (1, 3, 2):
            second[k, d].wait()

    def score_far(first_chunk, many):
        def step(i, carry):
            score_chunk(y_peer(2), first_chunk + i)
            return carry

        lax.fori_loop(0, many, step, 0)

    def hand_over(d):
        row_copies[d].wait()
        slot = lax.rem(y + SIDE - d, SIDE)
        part = rows.at[slot, shared, :]
        return remote(part, part, f_send.at[d], f_recv.at[d], (row, sibling))

    z_arrived(0)
    score_chunk(y, 0)
    near = [hand_over(1), hand_over(3)]
    z_arrived(1)
    score_chunk(y, 1)
    for copy in near:
        copy.wait()
    score_many(1, 2, 0, 2)
    far = hand_over(2)
    z_arrived(2)
    score_many(0, 3, 2, 1)
    far.wait()
    score_far(0, 3)
    z_arrived(3)
    score_many(0, 3, 3, 1)
    score_far(3, 1)
    for j in range(tiles):
        col_part[0, j:j + 1, :] = jnp.sum(col_acc[:, j * TILE:(j + 1) * TILE], axis=0, keepdims=True)

    def column_exchange(t):
        copies = []
        for d in (2, 1, 3):
            copies.append(
                remote(
                    col_part.at[t], col_in.at[t, z], c_send.at[t, d], c_recv.at[t, d],
                    (z_peer(d) * SIDE + y, me),
                )
            )
        col_in[t, z] = col_part[t]
        for copy in copies:
            copy.wait()
        column = 1.0 / (col_in[t, 0] + col_in[t, 1] + col_in[t, 2] + col_in[t, 3])
        for j in range(tiles):
            col16[:, j * TILE:(j + 1) * TILE] = stack16(column[j:j + 1, :])
            if t == ITERS - 1:
                colb[:, j * TILE:(j + 1) * TILE] = jnp.broadcast_to(column[j:j + 1, :], (8, TILE))

    def row_exchange(t):
        def to_sum(d, c):
            return pltpu.make_async_remote_copy(
                src_ref=row_mid.at[t], dst_ref=rowy_in.at[t, y],
                send_sem=y_send.at[t, d, c], recv_sem=y_recv.at[t, d],
                device_id=(z * SIDE + y_peer(d), chip * 2 + c), device_id_type=MESH,
            )

        to_odd = pltpu.make_async_remote_copy(
            src_ref=row_part.at[t], dst_ref=rowc_in.at[t], send_sem=s_send.at[t], recv_sem=s_recv.at[t],
            device_id=(row, sibling), device_id_type=MESH,
        )

        @pl.when(core == 0)
        def _():
            to_odd.start()
            to_odd.wait_send()
            for d in (0, 1, 3, 2):
                to_sum(d, 0).wait_recv()

        @pl.when(core == 1)
        def _():
            to_odd.wait_recv()
            pair = row_part[t] + rowc_in[t]
            row_pair[t] = pair
            copies = []
            for d in (2, 1, 3):
                copies.append(
                    remote(
                        row_pair.at[t], rowx_in.at[t, chip], x_send.at[t, d], x_recv.at[t, d],
                        (row, lax.rem(chip + d, SIDE) * 2 + core),
                    )
                )
            rowx_in[t, chip] = pair
            for copy in copies:
                copy.wait()
            total = rowx_in[t, 0] + rowx_in[t, 1] + rowx_in[t, 2] + rowx_in[t, 3]
            row_mid[t] = total
            copies = [to_sum(d, c) for d in (2, 1, 3) for c in (0, 1)] + [to_sum(0, 0)]
            for copy in copies:
                copy.start()
            rowy_in[t, y] = total
            for copy in copies:
                copy.wait_send()
            for d in (1, 3, 2):
                to_sum(d, 1).wait_recv()

        return rowy_in[t, 0] + rowy_in[t, 1] + rowy_in[t, 2] + rowy_in[t, 3]

    half = R // 2
    rid8, lane8 = iota((8, half), 0), iota((8, half), 1)
    spot = lax.rem(rid8, 2) * half + lane8
    queue_row = (z * SIDE + rid8 // 2) * Q + spot - B
    live = jnp.where(jnp.logical_or(spot < B, queue_row < fill), 1.0, 0.0)

    for t in range(ITERS):
        column_exchange(t)
        if t + 1 == ITERS:
            break

        for slot in range(SIDE):
            part = lax.dot_general(col16[...], mass[slot], NT, preferred_element_type=F32)
            part = jnp.sum(part, axis=0, keepdims=True)
            row_part[t, 2 * slot:2 * slot + 1, :] = part[:, 0:half]
            row_part[t, 2 * slot + 1:2 * slot + 2, :] = part[:, half:R]
        weight = live / row_exchange(t)
        for slot in range(SIDE):
            vector = jnp.concatenate(
                [weight[2 * slot:2 * slot + 1, :], weight[2 * slot + 1:2 * slot + 2, :]], axis=1
            )
            row16[slot] = stack16(vector)

        def column_tile(j, carry, t=t):
            cols = pl.ds(pl.multiple_of(j * TILE, TILE), TILE)
            part = jnp.dot(row16[0], mass[0, :, cols], preferred_element_type=F32)
            for slot in range(1, SIDE):
                part = part + jnp.dot(row16[slot], mass[slot, :, cols], preferred_element_type=F32)
            col_part[t + 1, pl.ds(j, 1), :] = jnp.sum(part, axis=0, keepdims=True)
            return carry

        lax.fori_loop(0, tiles, column_tile, 0)

    last = ITERS - 1
    for slot in range(SIDE):
        part = lax.dot_general(col16[...], mass[slot, 0:B, :], NT, preferred_element_type=F32)
        row_part[last, 2 * slot:2 * slot + 1, 0:B] = jnp.sum(part, axis=0, keepdims=True)
        row_part[last, 2 * slot + 1:2 * slot + 2, 0:B] = jnp.concatenate(
            [
                jnp.sum(soft_acc[slot, 0:128, :].T, axis=0, keepdims=True),
                jnp.sum(soft_acc[slot, 128:256, :].T, axis=0, keepdims=True),
            ],
            axis=1,
        )
        row_part[last, 2 * slot:2 * slot + 2, B:half] = jnp.ones((2, half - B), F32)
        eye = jnp.where(rid == cid, 1.0, 0.0).astype(BF16)
        turned[:, slot * B:(slot + 1) * B] = lax.dot_general(
            eye, rows[slot, 0:B, :], NT, preferred_element_type=F32
        ).astype(BF16)
    sums = row_exchange(last)
    for slot in range(SIDE):
        code = sums[2 * slot:2 * slot + 1, 0:B]
        soft = sums[2 * slot + 1:2 * slot + 2, 0:B]
        for target, value in ((row_code, (10.0 / (CROPS - 1)) / code), (row_soft, 10.0 / soft)):
            for h in range(2):
                target[slot, h * 128:(h + 1) * 128, :] = jnp.broadcast_to(
                    value[:, h * 128:(h + 1) * 128], (128, 128)
                ).T
    sublane = iota((8, B), 0)
    logs = jnp.log(sums[:, 0:B])
    mine = jnp.logical_and(sublane == 2 * y + 1, me == 0)
    logs = jnp.where(mine, logs, 0.0)
    logs = logs[:, 0:128] + logs[:, 128:256]

    images = B // CROPS
    slab = B // LANES

    def slope_chunk(slot, k, lost):
        for h in range(span // 128):
            lanes = pl.ds(pl.multiple_of(k * span + h * 128, 128), 128)
            column = colb[:, lanes]
            for i in range(images // 8):
                softs, parts, scores = [], [], []
                for c in range(CROPS):
                    at = slice(c * images + i * 8, c * images + i * 8 + 8)
                    s = score[slot, at, lanes]
                    e = jnp.exp2(s)
                    parts.append(e * e * column * row_code[slot, at, :])
                    softs.append(e * row_soft[slot, at, :])
                    scores.append(s)
                total = parts[0]
                for c in range(1, CROPS):
                    total = total + parts[c]
                for c in range(CROPS):
                    at = slice(c * images + i * 8, c * images + i * 8 + 8)
                    goal = total - parts[c]
                    lost = lost + goal * scores[c]
                    grad[slot, at, lanes] = (softs[c] - goal).astype(BF16)
        return lost

    def send_normed(n, slot):
        ng_out[n] = lax.dot_general(grad[slot], protos[...], NT, preferred_element_type=F32)
        copies = []
        for d in (4, 3, 5, 2, 6, 1, 7):
            to_p = p_peer(d)
            copies.append(
                remote(
                    ng_out.at[n, pl.ds(pl.multiple_of(to_p * slab, slab), slab), :],
                    ng_in.at[n, me], n_send.at[n, d], n_recv.at[n, d], (row, to_p),
                )
            )
        ng_in[n, me] = ng_out[n, pl.ds(pl.multiple_of(me * slab, slab), slab), :]
        return copies

    def sum_normed(n, copies):
        for copy in copies:
            copy.wait()
        total = ng_in[n, 0]
        for k in range(1, LANES):
            total = total + ng_in[n, k]
        return total

    def send_protos(k):
        for h in range(span // TILE):
            cols = slice(k * span + h * TILE, k * span + (h + 1) * TILE)
            part = jnp.dot(turned[:, 0:B], grad[0, :, cols], preferred_element_type=F32)
            for other in range(1, SIDE):
                part = part + jnp.dot(
                    turned[:, other * B:(other + 1) * B], grad[other, :, cols],
                    preferred_element_type=F32,
                )
            gp_out[:, cols] = part.astype(BF16)
        copies = []
        for dz, dy in (
            (2, 2), (2, 1), (2, 3), (1, 2), (3, 2), (1, 1), (1, 3), (3, 1), (3, 3),
            (2, 0), (0, 2), (1, 0), (3, 0), (0, 1), (0, 3),
        ):
            peer = z_peer(dz) * SIDE + y_peer(dy)
            m = len(copies)
            copies.append(
                remote(
                    gp_out.at[pl.ds(pl.multiple_of(peer * 16, 16), 16), k * span:(k + 1) * span],
                    gp_in.at[z, y, k], g_send.at[k, m], g_recv.at[k, m], (peer, me),
                )
            )
        return copies

    def pass_normed(n):
        ng_sum[n] = sum_normed(n, waiting[n])
        d = order[n]
        return remote(
            ng_sum.at[n], ngy_in.at[d], m_send.at[d], m_recv.at[d], (z * SIDE + y_peer(d), me)
        )

    order = (2, 1, 3, 0)
    lost = jnp.zeros((8, 128), F32)
    waiting, passing, gp_copies = [], [], []
    for n in range(SIDE):
        slot = y_peer(order[n])
        lost = lax.fori_loop(0, chunks, lambda k, lost, slot=slot: slope_chunk(slot, k, lost), lost)
        waiting.append(send_normed(n, slot))
    lx_in[me] = logs - lost * (math.log(2.0) / 10.0)
    loss_copies = []
    for d in range(1, LANES):
        loss_copies.append(
            remote(lx_in.at[me], lx_in.at[me], lx_send.at[d], lx_recv.at[d], (row, p_peer(d)))
        )
    gp_copies += send_protos(0)
    passing.append(pass_normed(0))
    gp_copies += send_protos(1)
    passing.append(pass_normed(1))
    for copy in loss_copies:
        copy.wait()
    lost = lx_in[0]
    for k in range(1, LANES):
        lost = lost + lx_in[k]
    lz_in[row] = lost
    loss_copies = []
    for dz in range(SIDE):
        for dy in range(SIDE):
            if dz or dy:
                m = len(loss_copies)
                loss_copies.append(
                    remote(
                        lz_in.at[row], lz_in.at[row], lz_send.at[m], lz_recv.at[m],
                        (z_peer(dz) * SIDE + y_peer(dy), me),
                    )
                )
    passing.append(pass_normed(2))
    gp_copies += send_protos(2)
    gp_copies += send_protos(3)
    total = sum_normed(3, waiting[3])
    for copy in passing:
        copy.wait()
    ng_all[me] = total + ngy_in[1] + ngy_in[2] + ngy_in[3]
    all_copies = []
    for d in (4, 3, 5, 2, 6, 1, 7):
        all_copies.append(
            remote(ng_all.at[me], ng_all.at[me], h_send.at[d], h_recv.at[d], (row, p_peer(d)))
        )

    for copy in all_copies:
        copy.wait()
    gathered = ng_all[...].reshape(B, D)
    normed_grad = jnp.zeros((B, D), F32)
    for term in split3(gathered):
        normed_grad = normed_grad + jnp.dot(back[...], term.astype(BF16), preferred_element_type=F32)
    along = jnp.sum(unit[...] * normed_grad, axis=1, keepdims=True)
    rest = normed_grad - unit[...] * along
    for h in range(D // 128):
        ge_ref[:, h * 128:(h + 1) * 128] = factor[...] * rest[:, h * 128:(h + 1) * 128]

    for copy in loss_copies:
        copy.wait()
    lost = lz_in[0]
    for k in range(1, SIDE * SIDE):
        lost = lost + lz_in[k]
    loss_ref[0] = jnp.sum(lost) * (1.0 / (B * SIDE * SIDE))

    for k in range(chunks):
        gp_in[z, y, k] = gp_out[dims, k * span:(k + 1) * span]
    for copy in gp_copies:
        copy.wait()
    for n in range(SIDE):
        for k in range(chunks):
            start = n * width + k * span
            gp_ref[:, start:start + span] = (
                gp_in[0, n, k].astype(F32) + gp_in[1, n, k].astype(F32)
                + gp_in[2, n, k].astype(F32) + gp_in[3, n, k].astype(F32)
            )


def body(embeddings, queue_feats, prototypes, crop_image, fill_count):
    width = prototypes.shape[1] // SIDE
    half = R // 2
    chunks = 4
    vmem = pl.BlockSpec(memory_space=pltpu.VMEM)
    smem = pl.BlockSpec(memory_space=pltpu.SMEM)
    dma = pltpu.SemaphoreType.DMA
    slab = B // LANES

    def pair(*shape):
        return [dma(shape), dma(shape)]

    scratch = [
        pltpu.VMEM((SIDE, R, D), BF16),
        pltpu.VMEM((D, width), BF16),
        pltpu.VMEM((SIDE, R, width), BF16),
        pltpu.VMEM((SIDE, B, width), F32),
        pltpu.VMEM((SIDE, B, width), BF16),
        pltpu.VMEM((D, SIDE * B), BF16),
        pltpu.VMEM((SIDE, B, 128), F32),
        pltpu.VMEM((8, width), F32),
        pltpu.VMEM((SIDE, Q, 128), F32),
        pltpu.VMEM((SIDE, 16, R), BF16),
        pltpu.VMEM((16, width), BF16),
        pltpu.VMEM((8, width), F32),
        pltpu.VMEM((ITERS, 8, width // 8), F32),
        pltpu.VMEM((ITERS, 8, half), F32),
        pltpu.VMEM((ITERS, 8, half), F32),
        pltpu.VMEM((ITERS, 8, half), F32),
        pltpu.VMEM((ITERS, SIDE, 8, width // 8), F32),
        pltpu.VMEM((ITERS, 8, half), F32),
        pltpu.VMEM((ITERS, SIDE, 8, half), F32),
        pltpu.VMEM((ITERS, SIDE, 8, half), F32),
        pltpu.VMEM((SIDE, B, 128), F32),
        pltpu.VMEM((SIDE, B, 128), F32),
        pltpu.VMEM((B, D), F32),
        pltpu.VMEM((B, 128), F32),
        pltpu.VMEM((B, B), BF16),
        pltpu.VMEM((D, width), BF16),
        pltpu.VMEM((SIDE, SIDE, chunks, 16, width // chunks), BF16),
        pltpu.VMEM((SIDE, B, D), F32),
        pltpu.VMEM((SIDE, LANES, slab, D), F32),
        pltpu.VMEM((SIDE, slab, D), F32),
        pltpu.VMEM((SIDE, slab, D), F32),
        pltpu.VMEM((LANES, slab, D), F32),
        pltpu.VMEM((LANES, 8, 128), F32),
        pltpu.VMEM((SIDE * SIDE, 8, 128), F32),
        *pair(chunks, SIDE), *pair(chunks, SIDE), *pair(SIDE), *pair(SIDE),
        *pair(ITERS, SIDE), *pair(ITERS), *pair(ITERS, SIDE),
        dma((ITERS, SIDE, 2)), dma((ITERS, SIDE)),
        *pair(chunks, 15), *pair(SIDE, LANES), *pair(SIDE), *pair(LANES),
        *pair(LANES), *pair(15),
    ]
    return pl.pallas_call(
        kernel,
        name="swav",
        out_shape=(
            pltpu.VMEM((B, D), F32),
            pltpu.VMEM((prototypes.shape[0], prototypes.shape[1]), F32),
            jax.ShapeDtypeStruct((1,), F32),
        ),
        in_specs=[smem, vmem, vmem, vmem, vmem],
        out_specs=(vmem, vmem, smem),
        scratch_shapes=scratch,
        compiler_params=pltpu.CompilerParams(
            collective_id=0, has_side_effects=True, vmem_limit_bytes=60 * 1024 * 1024
        ),
    )(fill_count, embeddings, queue_feats, prototypes, crop_image.reshape(1, B))


def solution(mesh):
    placed = (P("row", None), P("row", None), P("row", "proto"), P("row"), P())
    return jax.shard_map(
        body,
        mesh=mesh,
        in_specs=placed,
        out_specs=(P("row", None), P("row", "proto"), P()),
        check_vma=False,
    )
```

time: 131 us -> 108 us (0.82)
  Pallas kernels: 125 us -> 103 us
    pallas_call x1, Pallas kernels: 125 us -> 103 us  [body(): pl.pallas_call(kernel, name='swav', out_shape=(pltpu.VMEM((B, D), F32), p...]
where the time goes in v2:
time: 108 us
  Pallas kernels  103 us (95%)
  between operations  2.98 us (3%)
  local copies, waits for them, and re-layouts  1.5 us (1%)
    pallas_call x1, Pallas kernels, body(): pl.pallas_call(kernel, name='swav', out_shape=(pltpu.VMEM((B, D), F32), p...  103 us

profile of v2, /device:TPU:1, one launch (start us, length us, event | category | flops | bytes accessed | tf_op | source)
XLA Modules:
  0.0 107.7 jit_solution(7386269207530203952)
XLA Ops:
  1.3 103.2 %swav.1 = (f32[256,256]{1,0:T(8,128)S(1)}, f32[16,8192]{1,0:T(8,128)S(1)}, f32[1]{0:T(128)}) custom-call(s32[1]{0:T(128)S(6)} %copy.13.fill_ref, bf16[256,256]{1,0:T(8,128)(2,1)} %emb_ref.1, bf16[512,256]{1,0:T(8,128)(2,1)} %queue_ref.1, bf16[16,8192]{1,0:T(8,128)(2,1)} %proto_ref.1, s32[1,256]{1,0:T(1,128)} %bitcast.1), custom_call_target="tpu_custom_call" | custom-call | tf_op jit(solution)/shard_map/swav/pallas_call | solution.py:572
  104.5 0.7 copy.11
  105.2 0.8 copy.12

commit v3 on v2

--- a/solution.py
+++ b/solution.py
@@ -21,6 +21,7 @@
 B = 256
 Q = 512
 R = B + Q
+V = 512
 D = 256
 TILE = 256
 NT = (((1,), (1,)), ((), ()))
@@ -51,15 +52,15 @@
 
 
 def kernel(
-    fill_ref, emb_ref, queue_ref, proto_ref, image_ref,
+    fill_ref, emb_hbm, queue_hbm, proto_hbm, image_ref,
     ge_ref, gp_ref, loss_ref,
-    rows, protos, mass, score, grad, turned, soft_acc, col_acc, alive, row16, col16, colb,
+    emb_ref, queue_ref, proto_ref, rows, protos, massf, massb, row_acc, row_wide, score, grad, turned, soft_acc, col_acc, alive, row16, col16, colb,
     col_part, row_part, row_pair, row_mid, col_in, rowc_in, rowx_in, rowy_in,
     row_soft, row_code, unit, factor, back,
     gp_out, gp_in, ng_out, ng_in, ng_sum, ngy_in, ng_all, lx_in, lz_in,
     a_send, a_recv, z_send, z_recv, r_send, r_recv, f_send, f_recv,
     c_send, c_recv, s_send, s_recv, x_send, x_recv, y_send, y_recv,
-    g_send, g_recv, n_send, n_recv, m_send, m_recv, h_send, h_recv, lx_send, lx_recv, lz_send, lz_recv,
+    g_send, g_recv, n_send, n_recv, m_send, m_recv, h_send, h_recv, lx_send, lx_recv, lz_send, lz_recv, in_sem,
 ):
     row = lax.axis_index("row")
     me = lax.axis_index("proto")
@@ -90,6 +91,12 @@
         copy.start()
         return copy
 
+    loads = []
+    for n, (source, target) in enumerate(
+        ((emb_hbm, emb_ref), (queue_hbm, queue_ref), (proto_hbm, proto_ref))
+    ):
+        loads.append(pltpu.make_async_copy(source, target, in_sem.at[n]))
+        loads[-1].start()
     barrier = pltpu.get_barrier_semaphore()
     count = 0
     for dz in range(SIDE):
@@ -116,6 +123,8 @@
     base = (row * (B // CROPS)).astype(F32)
     place = jnp.sum(jnp.where(rid < cid, same, 0.0), axis=0, keepdims=True) * (B // CROPS) + (image - base)
     forward = jnp.where(rid.astype(F32) == place, 1.0, 0.0).astype(BF16)
+    for copy in loads:
+        copy.wait()
     exact, _ = unit_rows(emb_ref[...])
     ordered = jnp.dot(forward, exact.astype(BF16), preferred_element_type=F32).astype(BF16)
     rows[y, 0:B, :] = ordered
@@ -141,15 +150,21 @@
             (z * SIDE + y_peer(d), me),
         )
     second = {}
-    plane = pl.ds(pl.multiple_of(z * 64, 64), 64)
+
+    def to_z(k, source):
+        slot = lax.rem(y + SIDE - source, SIDE)
+        part = protos.at[pl.ds(pl.multiple_of((z * SIDE + slot) * 16, 16), 16), k * span:(k + 1) * span]
+        for d in (1, 3, 2):
+            second[k, source, d] = remote(
+                part, part, z_send.at[k, source, d], z_recv.at[k, source, d], (z_peer(d) * SIDE + y, me)
+            )
+
     for k in range(chunks):
-        for d in (1, 3, 2):
-            first[k, d].wait()
-        for d in (1, 3, 2):
-            part = protos.at[plane, k * span:(k + 1) * span]
-            second[k, d] = remote(
-                part, part, z_send.at[k, d], z_recv.at[k, d], (z_peer(d) * SIDE + y, me)
-            )
+        to_z(k, 0)
+    for k in range(chunks):
+        for source in (1, 3, 2):
+            first[k, source].wait()
+            to_z(k, source)
 
     soft_acc[...] = jnp.zeros_like(soft_acc)
     col_acc[...] = jnp.zeros_like(col_acc)
@@ -172,9 +187,10 @@
             soft = jnp.exp2(crop)
             soft_acc[slot] += soft[:, 0:128] + soft[:, 128:256]
             code = soft * soft
-            mass[slot, 0:B, cols] = code.astype(BF16)
+            massf[slot, 0:B, cols] = code
             rest = jnp.exp2(total[B:R] * (2.0 * SCALE))
-            mass[slot, B:R, cols] = rest.astype(BF16)
+            massf[slot, B:V, cols] = rest[0:V - B]
+            massb[slot, :, cols] = rest[V - B:].astype(BF16)
             live = alive[slot]
             for g in range(TILE // 128):
                 lanes = slice(g * 128, (g + 1) * 128)
@@ -192,8 +208,9 @@
         lax.fori_loop(0, slots * many, step, 0)
 
     def z_arrived(k):
-        for d in (1, 3, 2):
-            second[k, d].wait()
+        for source in range(SIDE):
+            for d in (1, 3, 2):
+                second[k, source, d].wait()
 
     def score_far(first_chunk, many):
         def step(i, carry):
@@ -242,8 +259,7 @@
         column = 1.0 / (col_in[t, 0] + col_in[t, 1] + col_in[t, 2] + col_in[t, 3])
         for j in range(tiles):
             col16[:, j * TILE:(j + 1) * TILE] = stack16(column[j:j + 1, :])
-            if t == ITERS - 1:
-                colb[:, j * TILE:(j + 1) * TILE] = jnp.broadcast_to(column[j:j + 1, :], (8, TILE))
+            colb[:, j * TILE:(j + 1) * TILE] = jnp.broadcast_to(column[j:j + 1, :], (8, TILE))
 
     def row_exchange(t):
         def to_sum(d, c):
@@ -294,6 +310,19 @@
 
         return rowy_in[t, 0] + rowy_in[t, 1] + rowy_in[t, 2] + rowy_in[t, 3]
 
+    def row_sums(slot, many):
+        for g in range(many // 8):
+            at = slice(g * 8, g * 8 + 8)
+            sums = [None, None]
+            for n in range(width // 128):
+                lanes = slice(n * 128, (n + 1) * 128)
+                term = massf[slot, at, lanes] * colb[:, lanes]
+                sums[n % 2] = term if sums[n % 2] is None else sums[n % 2] + term
+            row_acc[slot, at, :] = sums[0] + sums[1]
+
+    def turn(slot, b):
+        return jnp.sum(row_acc[slot, b * 128:(b + 1) * 128, :].T, axis=0, keepdims=True)
+
     half = R // 2
     rid8, lane8 = iota((8, half), 0), iota((8, half), 1)
     spot = lax.rem(rid8, 2) * half + lane8
@@ -305,32 +334,46 @@
         if t + 1 == ITERS:
             break
 
-        for slot in range(SIDE):
-            part = lax.dot_general(col16[...], mass[slot], NT, preferred_element_type=F32)
-            part = jnp.sum(part, axis=0, keepdims=True)
-            row_part[t, 2 * slot:2 * slot + 1, :] = part[:, 0:half]
-            row_part[t, 2 * slot + 1:2 * slot + 2, :] = part[:, half:R]
+        def row_block(slot, carry, t=t):
+            row_sums(slot, V)
+            rest = lax.dot_general(col16[...], massb[slot], NT, preferred_element_type=F32)
+            rest = jnp.sum(rest, axis=0, keepdims=True)
+            parts = [turn(slot, b) for b in range(V // 128)] + [rest[:, 0:128], rest[:, 128:256]]
+            for h in range(2):
+                row_part[t, pl.ds(2 * slot + h, 1), :] = jnp.concatenate(parts[3 * h:3 * h + 3], axis=1)
+            return carry
+
+        lax.fori_loop(0, SIDE, row_block, 0)
         weight = live / row_exchange(t)
         for slot in range(SIDE):
-            vector = jnp.concatenate(
-                [weight[2 * slot:2 * slot + 1, :], weight[2 * slot + 1:2 * slot + 2, :]], axis=1
-            )
-            row16[slot] = stack16(vector)
-
-        def column_tile(j, carry, t=t):
-            cols = pl.ds(pl.multiple_of(j * TILE, TILE), TILE)
-            part = jnp.dot(row16[0], mass[0, :, cols], preferred_element_type=F32)
-            for slot in range(1, SIDE):
-                part = part + jnp.dot(row16[slot], mass[slot, :, cols], preferred_element_type=F32)
-            col_part[t + 1, pl.ds(j, 1), :] = jnp.sum(part, axis=0, keepdims=True)
-            return carry
-
-        lax.fori_loop(0, tiles, column_tile, 0)
+            row16[slot] = stack16(weight[2 * slot + 1:2 * slot + 2, 128:half])
+            for b in range(V // 128):
+                at = slice((b % 3) * 128, (b % 3 + 1) * 128)
+                line = weight[2 * slot + b // 3:2 * slot + b // 3 + 1, at]
+                row_wide[slot, b * 128:(b + 1) * 128, :] = jnp.broadcast_to(line, (128, 128)).T
+
+        def column_block(slot, sums):
+            rest = jnp.dot(row16[slot], massb[slot], preferred_element_type=F32)
+            sums = list(sums)
+            for g in range(V // 8):
+                at = slice(g * 8, g * 8 + 8)
+                scale = row_wide[slot, at, :]
+                for n in range(width // 128):
+                    sums[n] = sums[n] + massf[slot, at, n * 128:(n + 1) * 128] * scale
+            return tuple(sums[n] + rest[0:8, n * 128:(n + 1) * 128] for n in range(width // 128))
+
+        sums = lax.fori_loop(
+            0, SIDE, column_block, tuple(jnp.zeros((8, 128), F32) for _ in range(width // 128))
+        )
+        for n in range(width // 128):
+            at = slice((n % 2) * 128, (n % 2 + 1) * 128)
+            col_part[t + 1, n // 2:n // 2 + 1, at] = jnp.sum(sums[n], axis=0, keepdims=True)
 
     last = ITERS - 1
     for slot in range(SIDE):
-        part = lax.dot_general(col16[...], mass[slot, 0:B, :], NT, preferred_element_type=F32)
-        row_part[last, 2 * slot:2 * slot + 1, 0:B] = jnp.sum(part, axis=0, keepdims=True)
+        row_sums(slot, B)
+        for b in range(B // 128):
+            row_part[last, 2 * slot:2 * slot + 1, b * 128:(b + 1) * 128] = turn(slot, b)
         row_part[last, 2 * slot + 1:2 * slot + 2, 0:B] = jnp.concatenate(
             [
                 jnp.sum(soft_acc[slot, 0:128, :].T, axis=0, keepdims=True),
@@ -455,6 +498,9 @@
     passing.append(pass_normed(0))
     gp_copies += send_protos(1)
     passing.append(pass_normed(1))
+    passing.append(pass_normed(2))
+    gp_copies += send_protos(2)
+    gp_copies += send_protos(3)
     for copy in loss_copies:
         copy.wait()
     lost = lx_in[0]
@@ -472,9 +518,6 @@
                         (z_peer(dz) * SIDE + y_peer(dy), me),
                     )
                 )
-    passing.append(pass_normed(2))
-    gp_copies += send_protos(2)
-    gp_copies += send_protos(3)
     total = sum_normed(3, waiting[3])
     for copy in passing:
         copy.wait()
@@ -522,6 +565,7 @@
     chunks = 4
     vmem = pl.BlockSpec(memory_space=pltpu.VMEM)
     smem = pl.BlockSpec(memory_space=pltpu.SMEM)
+    hbm = pl.BlockSpec(memory_space=pl.ANY)
     dma = pltpu.SemaphoreType.DMA
     slab = B // LANES
 
@@ -529,16 +573,22 @@
         return [dma(shape), dma(shape)]
 
     scratch = [
+        pltpu.VMEM((B, D), BF16),
+        pltpu.VMEM((Q, D), BF16),
+        pltpu.VMEM(prototypes.shape, BF16),
         pltpu.VMEM((SIDE, R, D), BF16),
         pltpu.VMEM((D, width), BF16),
-        pltpu.VMEM((SIDE, R, width), BF16),
+        pltpu.VMEM((SIDE, V, width), F32),
+        pltpu.VMEM((SIDE, R - V, width), BF16),
+        pltpu.VMEM((SIDE, V, 128), F32),
+        pltpu.VMEM((SIDE, V, 128), F32),
         pltpu.VMEM((SIDE, B, width), F32),
         pltpu.VMEM((SIDE, B, width), BF16),
         pltpu.VMEM((D, SIDE * B), BF16),
         pltpu.VMEM((SIDE, B, 128), F32),
         pltpu.VMEM((8, width), F32),
         pltpu.VMEM((SIDE, Q, 128), F32),
-        pltpu.VMEM((SIDE, 16, R), BF16),
+        pltpu.VMEM((SIDE, 16, R - V), BF16),
         pltpu.VMEM((16, width), BF16),
         pltpu.VMEM((8, width), F32),
         pltpu.VMEM((ITERS, 8, width // 8), F32),
@@ -563,11 +613,11 @@
         pltpu.VMEM((LANES, slab, D), F32),
         pltpu.VMEM((LANES, 8, 128), F32),
         pltpu.VMEM((SIDE * SIDE, 8, 128), F32),
-        *pair(chunks, SIDE), *pair(chunks, SIDE), *pair(SIDE), *pair(SIDE),
+        *pair(chunks, SIDE), *pair(chunks, SIDE, SIDE), *pair(SIDE), *pair(SIDE),
         *pair(ITERS, SIDE), *pair(ITERS), *pair(ITERS, SIDE),
         dma((ITERS, SIDE, 2)), dma((ITERS, SIDE)),
         *pair(chunks, 15), *pair(SIDE, LANES), *pair(SIDE), *pair(LANES),
-        *pair(LANES), *pair(15),
+        *pair(LANES), *pair(15), dma((3,)),
     ]
     return pl.pallas_call(
         kernel,
@@ -577,7 +627,7 @@
             pltpu.VMEM((prototypes.shape[0], prototypes.shape[1]), F32),
             jax.ShapeDtypeStruct((1,), F32),
         ),
-        in_specs=[smem, vmem, vmem, vmem, vmem],
+        in_specs=[smem, hbm, hbm, hbm, vmem],
         out_specs=(vmem, vmem, smem),
         scratch_shapes=scratch,
         compiler_params=pltpu.CompilerParams(

time: 108 us -> 101 us (0.935)
  Pallas kernels: 103 us -> 95.9 us
    pallas_call x1, Pallas kernels: 103 us -> 95.9 us  [body(): pl.pallas_call(kernel, name='swav', out_shape=(pltpu.VMEM((B, D), F32), p...]
where the time goes in v3:
time: 101 us; the launch traced here: 100 us
  Pallas kernels  95.9 us (95%)
  between operations  2.98 us (3%)
  local copies, waits for them, and re-layouts  1.5 us (1%)
    pallas_call x1, Pallas kernels, body(): pl.pallas_call(kernel, name='swav', out_shape=(pltpu.VMEM((B, D), F32), p...  95.9 us

profile of v3, /device:TPU:1, one launch (start us, length us, event | category | flops | bytes accessed | tf_op | source)
XLA Modules:
  0.0 100.4 jit_solution(2490089080240505845)
XLA Ops:
  1.3 95.9 %swav.1 = (f32[256,256]{1,0:T(8,128)S(1)}, f32[16,8192]{1,0:T(8,128)S(1)}, f32[1]{0:T(128)}) custom-call(s32[1]{0:T(128)S(6)} %copy.13.fill_ref, bf16[256,256]{1,0:T(8,128)(2,1)} %emb_hbm.1, bf16[512,256]{1,0:T(8,128)(2,1)} %queue_hbm.1, bf16[16,8192]{1,0:T(8,128)(2,1)} %proto_hbm.1, s32[1,256]{1,0:T(1,128)} %bitcast.1), custom_call_target="tpu_custom_call" | custom-call | tf_op jit(solution)/shard_map/swav/pallas_call | solution.py:622
  97.2 0.7 copy.11
  97.9 0.8 copy.12

commit v4 on v3

--- a/solution.py
+++ b/solution.py
@@ -55,11 +55,11 @@
     fill_ref, emb_hbm, queue_hbm, proto_hbm, image_ref,
     ge_ref, gp_ref, loss_ref,
     emb_ref, queue_ref, proto_ref, rows, protos, massf, massb, row_acc, row_wide, score, grad, turned, soft_acc, col_acc, alive, row16, col16, colb,
-    col_part, row_part, row_pair, row_mid, col_in, rowc_in, rowx_in, rowy_in,
+    col_part, row_part, row_mid, col_in, rowx_in, rowy_in,
     row_soft, row_code, unit, factor, back,
     gp_out, gp_in, ng_out, ng_in, ng_sum, ngy_in, ng_all, lx_in, lz_in,
     a_send, a_recv, z_send, z_recv, r_send, r_recv, f_send, f_recv,
-    c_send, c_recv, s_send, s_recv, x_send, x_recv, y_send, y_recv,
+    c_send, c_recv, x_send, x_recv, y_send, y_recv,
     g_send, g_recv, n_send, n_recv, m_send, m_recv, h_send, h_recv, lx_send, lx_recv, lz_send, lz_recv, in_sem,
 ):
     row = lax.axis_index("row")
@@ -90,6 +90,18 @@
         )
         copy.start()
         return copy
+
+    def landed(ref, recv):
+        pltpu.make_async_remote_copy(
+            src_ref=ref, dst_ref=ref, send_sem=recv, recv_sem=recv,
+            device_id=(row, sibling), device_id_type=MESH,
+        ).wait_recv()
+
+    def left(ref, send):
+        pltpu.make_async_remote_copy(
+            src_ref=ref, dst_ref=ref, send_sem=send, recv_sem=send,
+            device_id=(row, sibling), device_id_type=MESH,
+        ).wait_send()
 
     loads = []
     for n, (source, target) in enumerate(
@@ -134,36 +146,37 @@
 
     pl.semaphore_wait(barrier, count)
 
-    first = {}
+    def from_y(k, d):
+        return pltpu.make_async_remote_copy(
+            src_ref=protos.at[dims, k * span:(k + 1) * span],
+            dst_ref=protos.at[dims, k * span:(k + 1) * span],
+            send_sem=a_send, recv_sem=a_recv.at[k, d], device_id=(row, sibling), device_id_type=MESH,
+        )
+
     for k in range(chunks):
         for d in (1, 3, 2):
-            first[k, d] = remote(
+            remote(
                 proto_ref.at[:, pl.ds(pl.multiple_of(y_peer(d) * width + k * span, span), span)],
-                protos.at[dims, k * span:(k + 1) * span], a_send.at[k, d], a_recv.at[k, d],
+                protos.at[dims, k * span:(k + 1) * span], a_send, a_recv.at[k, d],
                 (z * SIDE + y_peer(d), me),
             )
     shared = pl.ds(pl.multiple_of(core * (R // 2), R // 2), R // 2)
-    row_copies = {}
     for d in (1, 3, 2):
-        row_copies[d] = remote(
-            rows.at[y, shared, :], rows.at[y, shared, :], r_send.at[d], r_recv.at[d],
+        remote(
+            rows.at[y, shared, :], rows.at[y, shared, :], r_send, r_recv.at[d],
             (z * SIDE + y_peer(d), me),
         )
-    second = {}
-
     def to_z(k, source):
         slot = lax.rem(y + SIDE - source, SIDE)
         part = protos.at[pl.ds(pl.multiple_of((z * SIDE + slot) * 16, 16), 16), k * span:(k + 1) * span]
         for d in (1, 3, 2):
-            second[k, source, d] = remote(
-                part, part, z_send.at[k, source, d], z_recv.at[k, source, d], (z_peer(d) * SIDE + y, me)
-            )
+            remote(part, part, z_send, z_recv.at[k], (z_peer(d) * SIDE + y, me))
 
     for k in range(chunks):
         to_z(k, 0)
     for k in range(chunks):
         for source in (1, 3, 2):
-            first[k, source].wait()
+            from_y(k, source).wait_recv()
             to_z(k, source)
 
     soft_acc[...] = jnp.zeros_like(soft_acc)
@@ -208,9 +221,7 @@
         lax.fori_loop(0, slots * many, step, 0)
 
     def z_arrived(k):
-        for source in range(SIDE):
-            for d in (1, 3, 2):
-                second[k, source, d].wait()
+        landed(protos.at[0:192, 0:span], z_recv.at[k])
 
     def score_far(first_chunk, many):
         def step(i, carry):
@@ -220,23 +231,24 @@
         lax.fori_loop(0, many, step, 0)
 
     def hand_over(d):
-        row_copies[d].wait()
+        landed(rows.at[0, 0:R // 2, :], r_recv.at[d])
         slot = lax.rem(y + SIDE - d, SIDE)
         part = rows.at[slot, shared, :]
-        return remote(part, part, f_send.at[d], f_recv.at[d], (row, sibling))
+        remote(part, part, f_send, f_recv.at[d], (row, sibling))
 
     z_arrived(0)
     score_chunk(y, 0)
-    near = [hand_over(1), hand_over(3)]
+    hand_over(1)
+    hand_over(3)
     z_arrived(1)
     score_chunk(y, 1)
-    for copy in near:
-        copy.wait()
+    landed(rows.at[0, 0:R // 2, :], f_recv.at[1])
+    landed(rows.at[0, 0:R // 2, :], f_recv.at[3])
     score_many(1, 2, 0, 2)
-    far = hand_over(2)
+    hand_over(2)
     z_arrived(2)
     score_many(0, 3, 2, 1)
-    far.wait()
+    landed(rows.at[0, 0:R // 2, :], f_recv.at[2])
     score_far(0, 3)
     z_arrived(3)
     score_many(0, 3, 3, 1)
@@ -245,68 +257,44 @@
         col_part[0, j:j + 1, :] = jnp.sum(col_acc[:, j * TILE:(j + 1) * TILE], axis=0, keepdims=True)
 
     def column_exchange(t):
-        copies = []
         for d in (2, 1, 3):
-            copies.append(
-                remote(
-                    col_part.at[t], col_in.at[t, z], c_send.at[t, d], c_recv.at[t, d],
-                    (z_peer(d) * SIDE + y, me),
-                )
+            remote(
+                col_part.at[t], col_in.at[t, z], c_send, c_recv.at[t], (z_peer(d) * SIDE + y, me)
             )
         col_in[t, z] = col_part[t]
-        for copy in copies:
-            copy.wait()
+        landed(col_in.at[t, 0:SIDE - 1], c_recv.at[t])
         column = 1.0 / (col_in[t, 0] + col_in[t, 1] + col_in[t, 2] + col_in[t, 3])
         for j in range(tiles):
             col16[:, j * TILE:(j + 1) * TILE] = stack16(column[j:j + 1, :])
             colb[:, j * TILE:(j + 1) * TILE] = jnp.broadcast_to(column[j:j + 1, :], (8, TILE))
 
     def row_exchange(t):
-        def to_sum(d, c):
-            return pltpu.make_async_remote_copy(
-                src_ref=row_mid.at[t], dst_ref=rowy_in.at[t, y],
-                send_sem=y_send.at[t, d, c], recv_sem=y_recv.at[t, d],
-                device_id=(z * SIDE + y_peer(d), chip * 2 + c), device_id_type=MESH,
+        for d in (2, 1, 3):
+            remote(
+                row_part.at[t], rowx_in.at[t, me], x_send, x_recv.at[t],
+                (row, lax.rem(chip + d, SIDE) * 2 + 1),
             )
-
-        to_odd = pltpu.make_async_remote_copy(
-            src_ref=row_part.at[t], dst_ref=rowc_in.at[t], send_sem=s_send.at[t], recv_sem=s_recv.at[t],
-            device_id=(row, sibling), device_id_type=MESH,
-        )
 
         @pl.when(core == 0)
         def _():
-            to_odd.start()
-            to_odd.wait_send()
-            for d in (0, 1, 3, 2):
-                to_sum(d, 0).wait_recv()
+            remote(row_part.at[t], rowx_in.at[t, me], x_send, x_recv.at[t], (row, sibling))
+            landed(rowy_in.at[t], y_recv.at[t])
 
         @pl.when(core == 1)
         def _():
-            to_odd.wait_recv()
-            pair = row_part[t] + rowc_in[t]
-            row_pair[t] = pair
-            copies = []
-            for d in (2, 1, 3):
-                copies.append(
-                    remote(
-                        row_pair.at[t], rowx_in.at[t, chip], x_send.at[t, d], x_recv.at[t, d],
-                        (row, lax.rem(chip + d, SIDE) * 2 + core),
-                    )
+            rowx_in[t, me] = row_part[t]
+            landed(rowx_in.at[t, 0:LANES - 1], x_recv.at[t])
+            total = rowx_in[t, 0]
+            for k in range(1, LANES):
+                total = total + rowx_in[t, k]
+            row_mid[t] = total
+            for d, c in ((2, 0), (2, 1), (1, 0), (1, 1), (3, 0), (3, 1), (0, 0)):
+                remote(
+                    row_mid.at[t], rowy_in.at[t, y], y_send, y_recv.at[t],
+                    (z * SIDE + y_peer(d), chip * 2 + c),
                 )
-            rowx_in[t, chip] = pair
-            for copy in copies:
-                copy.wait()
-            total = rowx_in[t, 0] + rowx_in[t, 1] + rowx_in[t, 2] + rowx_in[t, 3]
-            row_mid[t] = total
-            copies = [to_sum(d, c) for d in (2, 1, 3) for c in (0, 1)] + [to_sum(0, 0)]
-            for copy in copies:
-                copy.start()
             rowy_in[t, y] = total
-            for copy in copies:
-                copy.wait_send()
-            for d in (1, 3, 2):
-                to_sum(d, 1).wait_recv()
+            landed(rowy_in.at[t, 0:SIDE - 1], y_recv.at[t])
 
         return rowy_in[t, 0] + rowy_in[t, 1] + rowy_in[t, 2] + rowy_in[t, 3]
 
@@ -429,21 +417,16 @@
 
     def send_normed(n, slot):
         ng_out[n] = lax.dot_general(grad[slot], protos[...], NT, preferred_element_type=F32)
-        copies = []
         for d in (4, 3, 5, 2, 6, 1, 7):
             to_p = p_peer(d)
-            copies.append(
-                remote(
-                    ng_out.at[n, pl.ds(pl.multiple_of(to_p * slab, slab), slab), :],
-                    ng_in.at[n, me], n_send.at[n, d], n_recv.at[n, d], (row, to_p),
-                )
+            remote(
+                ng_out.at[n, pl.ds(pl.multiple_of(to_p * slab, slab), slab), :],
+                ng_in.at[n, me], n_send, n_recv.at[n], (row, to_p),
             )
         ng_in[n, me] = ng_out[n, pl.ds(pl.multiple_of(me * slab, slab), slab), :]
-        return copies
-
-    def sum_normed(n, copies):
-        for copy in copies:
-            copy.wait()
+
+    def sum_normed(n):
+        landed(ng_in.at[n, 0:LANES - 1], n_recv.at[n])
         total = ng_in[n, 0]
         for k in range(1, LANES):
             total = total + ng_in[n, k]
@@ -459,77 +442,56 @@
                     preferred_element_type=F32,
                 )
             gp_out[:, cols] = part.astype(BF16)
-        copies = []
         for dz, dy in (
             (2, 2), (2, 1), (2, 3), (1, 2), (3, 2), (1, 1), (1, 3), (3, 1), (3, 3),
             (2, 0), (0, 2), (1, 0), (3, 0), (0, 1), (0, 3),
         ):
             peer = z_peer(dz) * SIDE + y_peer(dy)
-            m = len(copies)
-            copies.append(
-                remote(
-                    gp_out.at[pl.ds(pl.multiple_of(peer * 16, 16), 16), k * span:(k + 1) * span],
-                    gp_in.at[z, y, k], g_send.at[k, m], g_recv.at[k, m], (peer, me),
-                )
+            remote(
+                gp_out.at[pl.ds(pl.multiple_of(peer * 16, 16), 16), k * span:(k + 1) * span],
+                gp_in.at[z, y, k], g_send, g_recv, (peer, me),
             )
-        return copies
 
     def pass_normed(n):
-        ng_sum[n] = sum_normed(n, waiting[n])
+        ng_sum[n] = sum_normed(n)
         d = order[n]
-        return remote(
-            ng_sum.at[n], ngy_in.at[d], m_send.at[d], m_recv.at[d], (z * SIDE + y_peer(d), me)
-        )
+        remote(ng_sum.at[n], ngy_in.at[d], m_send, m_recv, (z * SIDE + y_peer(d), me))
 
     order = (2, 1, 3, 0)
     lost = jnp.zeros((8, 128), F32)
-    waiting, passing, gp_copies = [], [], []
     for n in range(SIDE):
         slot = y_peer(order[n])
         lost = lax.fori_loop(0, chunks, lambda k, lost, slot=slot: slope_chunk(slot, k, lost), lost)
-        waiting.append(send_normed(n, slot))
-    lx_in[me] = logs - lost * (math.log(2.0) / 10.0)
-    loss_copies = []
-    for d in range(1, LANES):
-        loss_copies.append(
-            remote(lx_in.at[me], lx_in.at[me], lx_send.at[d], lx_recv.at[d], (row, p_peer(d)))
-        )
-    gp_copies += send_protos(0)
-    passing.append(pass_normed(0))
-    gp_copies += send_protos(1)
-    passing.append(pass_normed(1))
-    passing.append(pass_normed(2))
-    gp_copies += send_protos(2)
-    gp_copies += send_protos(3)
-    for copy in loss_copies:
-        copy.wait()
+        if n == SIDE - 1:
+            lx_in[me] = logs - lost * (math.log(2.0) / 10.0)
+            for d in range(1, LANES):
+                remote(lx_in.at[me], lx_in.at[me], lx_send, lx_recv, (row, p_peer(d)))
+        send_normed(n, slot)
+    send_protos(0)
+    pass_normed(0)
+    send_protos(1)
+    pass_normed(1)
+    pass_normed(2)
+    landed(lx_in.at[0:LANES - 1], lx_recv)
     lost = lx_in[0]
     for k in range(1, LANES):
         lost = lost + lx_in[k]
     lz_in[row] = lost
-    loss_copies = []
     for dz in range(SIDE):
         for dy in range(SIDE):
             if dz or dy:
-                m = len(loss_copies)
-                loss_copies.append(
-                    remote(
-                        lz_in.at[row], lz_in.at[row], lz_send.at[m], lz_recv.at[m],
-                        (z_peer(dz) * SIDE + y_peer(dy), me),
-                    )
+                remote(
+                    lz_in.at[row], lz_in.at[row], lz_send, lz_recv, (z_peer(dz) * SIDE + y_peer(dy), me)
                 )
-    total = sum_normed(3, waiting[3])
-    for copy in passing:
-        copy.wait()
+    send_protos(2)
+    send_protos(3)
+    total = sum_normed(3)
+    landed(ngy_in.at[0:SIDE - 1], m_recv)
     ng_all[me] = total + ngy_in[1] + ngy_in[2] + ngy_in[3]
-    all_copies = []
     for d in (4, 3, 5, 2, 6, 1, 7):
-        all_copies.append(
-            remote(ng_all.at[me], ng_all.at[me], h_send.at[d], h_recv.at[d], (row, p_peer(d)))
-        )
-
-    for copy in all_copies:
-        copy.wait()
+        remote(ng_all.at[me], ng_all.at[me], h_send, h_recv, (row, p_peer(d)))
+
+    landed(ng_all.at[0:LANES - 1], h_recv)
     gathered = ng_all[...].reshape(B, D)
     normed_grad = jnp.zeros((B, D), F32)
     for term in split3(gathered):
@@ -539,8 +501,7 @@
     for h in range(D // 128):
         ge_ref[:, h * 128:(h + 1) * 128] = factor[...] * rest[:, h * 128:(h + 1) * 128]
 
-    for copy in loss_copies:
-        copy.wait()
+    landed(lz_in.at[0:SIDE * SIDE - 1], lz_recv)
     lost = lz_in[0]
     for k in range(1, SIDE * SIDE):
         lost = lost + lz_in[k]
@@ -548,8 +509,7 @@
 
     for k in range(chunks):
         gp_in[z, y, k] = gp_out[dims, k * span:(k + 1) * span]
-    for copy in gp_copies:
-        copy.wait()
+    landed(gp_out.at[0:240, :], g_recv)
     for n in range(SIDE):
         for k in range(chunks):
             start = n * width + k * span
@@ -557,6 +517,26 @@
                 gp_in[0, n, k].astype(F32) + gp_in[1, n, k].astype(F32)
                 + gp_in[2, n, k].astype(F32) + gp_in[3, n, k].astype(F32)
             )
+    left(protos.at[0:192, 0:span], a_send)
+    left(protos.at[0:192, :], z_send)
+    left(rows.at[0:3, 0:R // 2, :], r_send)
+    left(rows.at[0:3, 0:R // 2, :], f_send)
+    left(col_in.at[:, 0:SIDE - 1], c_send)
+    left(gp_out.at[0:240, :], g_send)
+    left(ng_in.at[:, 0:LANES - 1], n_send)
+    left(ngy_in.at[0:SIDE - 1], m_send)
+    left(ng_all.at[0:LANES - 1], h_send)
+    left(lx_in.at[0:LANES - 1], lx_send)
+    left(lz_in.at[0:SIDE * SIDE - 1], lz_send)
+
+    @pl.when(core == 0)
+    def _():
+        left(rowx_in.at[:, 0:SIDE], x_send)
+
+    @pl.when(core == 1)
+    def _():
+        left(rowx_in.at[:, 0:SIDE - 1], x_send)
+        left(rowx_in.at[:, 0:LANES - 1], y_send)
 
 
 def body(embeddings, queue_feats, prototypes, crop_image, fill_count):
@@ -569,8 +549,8 @@
     dma = pltpu.SemaphoreType.DMA
     slab = B // LANES
 
-    def pair(*shape):
-        return [dma(shape), dma(shape)]
+    def group(*shape):
+        return [dma, dma(shape) if shape else dma]
 
     scratch = [
         pltpu.VMEM((B, D), BF16),
@@ -594,10 +574,8 @@
         pltpu.VMEM((ITERS, 8, width // 8), F32),
         pltpu.VMEM((ITERS, 8, half), F32),
         pltpu.VMEM((ITERS, 8, half), F32),
-        pltpu.VMEM((ITERS, 8, half), F32),
         pltpu.VMEM((ITERS, SIDE, 8, width // 8), F32),
-        pltpu.VMEM((ITERS, 8, half), F32),
-        pltpu.VMEM((ITERS, SIDE, 8, half), F32),
+        pltpu.VMEM((ITERS, LANES, 8, half), F32),
         pltpu.VMEM((ITERS, SIDE, 8, half), F32),
         pltpu.VMEM((SIDE, B, 128), F32),
         pltpu.VMEM((SIDE, B, 128), F32),
@@ -613,11 +591,9 @@
         pltpu.VMEM((LANES, slab, D), F32),
         pltpu.VMEM((LANES, 8, 128), F32),
         pltpu.VMEM((SIDE * SIDE, 8, 128), F32),
-        *pair(chunks, SIDE), *pair(chunks, SIDE, SIDE), *pair(SIDE), *pair(SIDE),
-        *pair(ITERS, SIDE), *pair(ITERS), *pair(ITERS, SIDE),
-        dma((ITERS, SIDE, 2)), dma((ITERS, SIDE)),
-        *pair(chunks, 15), *pair(SIDE, LANES), *pair(SIDE), *pair(LANES),
-        *pair(LANES), *pair(15), dma((3,)),
+        *group(chunks, SIDE), *group(chunks), *group(SIDE), *group(SIDE),
+        *group(ITERS), *group(ITERS), *group(ITERS),
+        *group(), *group(SIDE), *group(), *group(), *group(), *group(), dma((3,)),
     ]
     return pl.pallas_call(
         kernel,

time: 101 us -> 94.7 us (0.938)
  Pallas kernels: 95.9 us -> 90 us
    pallas_call x1, Pallas kernels: 95.9 us -> 90 us  [body(): pl.pallas_call(kernel, name='swav', out_shape=(pltpu.VMEM((B, D), F32), p...]
where the time goes in v4:
time: 94.7 us; the launch traced here: 94.5 us
  Pallas kernels  90 us (95%)
  between operations  2.98 us (3%)
  local copies, waits for them, and re-layouts  1.5 us (2%)
    pallas_call x1, Pallas kernels, body(): pl.pallas_call(kernel, name='swav', out_shape=(pltpu.VMEM((B, D), F32), p...  90 us

profile of v4, /device:TPU:1, one launch (start us, length us, event | category | flops | bytes accessed | tf_op | source)
XLA Modules:
  0.0 94.5 jit_solution(11130420849140379868)
XLA Ops:
  1.3 90.0 %swav.1 = (f32[256,256]{1,0:T(8,128)S(1)}, f32[16,8192]{1,0:T(8,128)S(1)}, f32[1]{0:T(128)}) custom-call(s32[1]{0:T(128)S(6)} %copy.13.fill_ref, bf16[256,256]{1,0:T(8,128)(2,1)} %emb_hbm.1, bf16[512,256]{1,0:T(8,128)(2,1)} %queue_hbm.1, bf16[16,8192]{1,0:T(8,128)(2,1)} %proto_hbm.1, s32[1,256]{1,0:T(1,128)} %bitcast.1), custom_call_target="tpu_custom_call" | custom-call | tf_op jit(solution)/shard_map/swav/pallas_call | solution.py:598
  91.3 0.7 copy.11
  92.0 0.8 copy.12

commit v5 on v4

--- a/solution.py
+++ b/solution.py
@@ -57,10 +57,10 @@
     emb_ref, queue_ref, proto_ref, rows, protos, massf, massb, row_acc, row_wide, score, grad, turned, soft_acc, col_acc, alive, row16, col16, colb,
     col_part, row_part, row_mid, col_in, rowx_in, rowy_in,
     row_soft, row_code, unit, factor, back,
-    gp_out, gp_in, ng_out, ng_in, ng_sum, ngy_in, ng_all, lx_in, lz_in,
+    gp_out, gp_in, ng_out, ngc_in, ng_pair, ng_in, ng_sum, ngy_in, ng_all, lx_in, lz_in,
     a_send, a_recv, z_send, z_recv, r_send, r_recv, f_send, f_recv,
     c_send, c_recv, x_send, x_recv, y_send, y_recv,
-    g_send, g_recv, n_send, n_recv, m_send, m_recv, h_send, h_recv, lx_send, lx_recv, lz_send, lz_recv, in_sem,
+    g_send, g_recv, e_send, e_recv, n_send, n_recv, m_send, m_recv, h_send, h_recv, lx_send, lx_recv, lz_send, lz_recv, in_sem,
 ):
     row = lax.axis_index("row")
     me = lax.axis_index("proto")
@@ -111,20 +111,12 @@
         loads[-1].start()
     barrier = pltpu.get_barrier_semaphore()
     count = 0
-    for dz in range(SIDE):
-        for dy in range(SIDE):
-            if dz or dy:
-                pl.semaphore_signal(
-                    barrier, inc=1, device_id=(z_peer(dz) * SIDE + y_peer(dy), me), device_id_type=MESH
-                )
-                count += 1
-    for dp in range(1, LANES):
-        pl.semaphore_signal(barrier, inc=1, device_id=(row, p_peer(dp)), device_id_type=MESH)
-        count += 1
-    for dy in range(1, SIDE):
-        pl.semaphore_signal(
-            barrier, inc=1, device_id=(z * SIDE + y_peer(dy), sibling), device_id_type=MESH
-        )
+    for d in range(1, SIDE):
+        for peer in (z * SIDE + y_peer(d), z_peer(d) * SIDE + y):
+            pl.semaphore_signal(barrier, inc=1, device_id=(peer, me), device_id_type=MESH)
+            count += 1
+    for d in range(1, LANES):
+        pl.semaphore_signal(barrier, inc=1, device_id=(row, p_peer(d)), device_id_type=MESH)
         count += 1
 
     image = image_ref[...].astype(F32)
@@ -248,11 +240,10 @@
     hand_over(2)
     z_arrived(2)
     score_many(0, 3, 2, 1)
-    landed(rows.at[0, 0:R // 2, :], f_recv.at[2])
-    score_far(0, 3)
     z_arrived(3)
     score_many(0, 3, 3, 1)
-    score_far(3, 1)
+    landed(rows.at[0, 0:R // 2, :], f_recv.at[2])
+    score_far(0, chunks)
     for j in range(tiles):
         col_part[0, j:j + 1, :] = jnp.sum(col_acc[:, j * TILE:(j + 1) * TILE], axis=0, keepdims=True)
 
@@ -415,22 +406,31 @@
                     grad[slot, at, lanes] = (softs[c] - goal).astype(BF16)
         return lost
 
-    def send_normed(n, slot):
-        ng_out[n] = lax.dot_general(grad[slot], protos[...], NT, preferred_element_type=F32)
-        for d in (4, 3, 5, 2, 6, 1, 7):
-            to_p = p_peer(d)
+    def normed_chunk(slot, k):
+        cols = pl.ds(pl.multiple_of(k * span, span), span)
+        return lax.dot_general(grad[slot, :, cols], protos[:, cols], NT, preferred_element_type=F32)
+
+    side = B // 2
+    own_half = pl.ds(pl.multiple_of(core * side, side), side)
+    other_half = pl.ds(pl.multiple_of((1 - core) * side, side), side)
+
+    def to_sibling(n):
+        remote(ng_out.at[n, other_half, :], ngc_in.at[n], e_send, e_recv.at[n], (row, sibling))
+
+    def to_chips(n):
+        landed(ngc_in.at[n], e_recv.at[n])
+        ng_pair[n] = ng_out[n, own_half, :] + ngc_in[n]
+        for d in (2, 1, 3):
+            to_chip = lax.rem(chip + d, SIDE)
             remote(
-                ng_out.at[n, pl.ds(pl.multiple_of(to_p * slab, slab), slab), :],
-                ng_in.at[n, me], n_send, n_recv.at[n], (row, to_p),
+                ng_pair.at[n, pl.ds(pl.multiple_of(to_chip * slab, slab), slab), :],
+                ng_in.at[n, chip], n_send, n_recv.at[n], (row, to_chip * 2 + core),
             )
-        ng_in[n, me] = ng_out[n, pl.ds(pl.multiple_of(me * slab, slab), slab), :]
+        ng_in[n, chip] = ng_pair[n, pl.ds(pl.multiple_of(chip * slab, slab), slab), :]
 
     def sum_normed(n):
-        landed(ng_in.at[n, 0:LANES - 1], n_recv.at[n])
-        total = ng_in[n, 0]
-        for k in range(1, LANES):
-            total = total + ng_in[n, k]
-        return total
+        landed(ng_in.at[n, 0:SIDE - 1], n_recv.at[n])
+        return ng_in[n, 0] + ng_in[n, 1] + ng_in[n, 2] + ng_in[n, 3]
 
     def send_protos(k):
         for h in range(span // TILE):
@@ -461,15 +461,30 @@
     lost = jnp.zeros((8, 128), F32)
     for n in range(SIDE):
         slot = y_peer(order[n])
-        lost = lax.fori_loop(0, chunks, lambda k, lost, slot=slot: slope_chunk(slot, k, lost), lost)
-        if n == SIDE - 1:
-            lx_in[me] = logs - lost * (math.log(2.0) / 10.0)
-            for d in range(1, LANES):
-                remote(lx_in.at[me], lx_in.at[me], lx_send, lx_recv, (row, p_peer(d)))
-        send_normed(n, slot)
+        if n:
+            ng_out[n - 1] = jnp.zeros((B, D), F32)
+
+        def block_chunk(k, lost, n=n, slot=slot):
+            lost = slope_chunk(slot, k, lost)
+            if n:
+                ng_out[n - 1] += normed_chunk(y_peer(order[n - 1]), k)
+            return lost
+
+        lost = lax.fori_loop(0, chunks, block_chunk, lost)
+        if n >= 1:
+            to_sibling(n - 1)
+        if n >= 2:
+            to_chips(n - 2)
+    lx_in[me] = logs - lost * (math.log(2.0) / 10.0)
+    for d in range(1, LANES):
+        remote(lx_in.at[me], lx_in.at[me], lx_send, lx_recv, (row, p_peer(d)))
+    ng_out[SIDE - 1] = lax.dot_general(grad[y], protos[...], NT, preferred_element_type=F32)
+    to_sibling(SIDE - 1)
+    to_chips(SIDE - 2)
     send_protos(0)
+    to_chips(SIDE - 1)
+    send_protos(1)
     pass_normed(0)
-    send_protos(1)
     pass_normed(1)
     pass_normed(2)
     landed(lx_in.at[0:LANES - 1], lx_recv)
@@ -487,9 +502,10 @@
     send_protos(3)
     total = sum_normed(3)
     landed(ngy_in.at[0:SIDE - 1], m_recv)
-    ng_all[me] = total + ngy_in[1] + ngy_in[2] + ngy_in[3]
+    mine_at = core * SIDE + chip
+    ng_all[mine_at] = total + ngy_in[1] + ngy_in[2] + ngy_in[3]
     for d in (4, 3, 5, 2, 6, 1, 7):
-        remote(ng_all.at[me], ng_all.at[me], h_send, h_recv, (row, p_peer(d)))
+        remote(ng_all.at[mine_at], ng_all.at[mine_at], h_send, h_recv, (row, p_peer(d)))
 
     landed(ng_all.at[0:LANES - 1], h_recv)
     gathered = ng_all[...].reshape(B, D)
@@ -523,7 +539,8 @@
     left(rows.at[0:3, 0:R // 2, :], f_send)
     left(col_in.at[:, 0:SIDE - 1], c_send)
     left(gp_out.at[0:240, :], g_send)
-    left(ng_in.at[:, 0:LANES - 1], n_send)
+    left(ng_in.at[:, 0:SIDE - 1], n_send)
+    left(ngc_in, e_send)
     left(ngy_in.at[0:SIDE - 1], m_send)
     left(ng_all.at[0:LANES - 1], h_send)
     left(lx_in.at[0:LANES - 1], lx_send)
@@ -585,7 +602,9 @@
         pltpu.VMEM((D, width), BF16),
         pltpu.VMEM((SIDE, SIDE, chunks, 16, width // chunks), BF16),
         pltpu.VMEM((SIDE, B, D), F32),
-        pltpu.VMEM((SIDE, LANES, slab, D), F32),
+        pltpu.VMEM((SIDE, B // 2, D), F32),
+        pltpu.VMEM((SIDE, B // 2, D), F32),
+        pltpu.VMEM((SIDE, SIDE, slab, D), F32),
         pltpu.VMEM((SIDE, slab, D), F32),
         pltpu.VMEM((SIDE, slab, D), F32),
         pltpu.VMEM((LANES, slab, D), F32),
@@ -593,7 +612,7 @@
         pltpu.VMEM((SIDE * SIDE, 8, 128), F32),
         *group(chunks, SIDE), *group(chunks), *group(SIDE), *group(SIDE),
         *group(ITERS), *group(ITERS), *group(ITERS),
-        *group(), *group(SIDE), *group(), *group(), *group(), *group(), dma((3,)),
+        *group(), *group(SIDE), *group(SIDE), *group(), *group(), *group(), *group(), dma((3,)),
     ]
     return pl.pallas_call(
         kernel,

time: 94.7 us -> 95.5 us (level)
  no operation moved by 1% of the time
where the time goes in v5:
time: 95.5 us; the launch traced here: 95.3 us
  Pallas kernels  90.9 us (95%)
  between operations  2.98 us (3%)
  local copies, waits for them, and re-layouts  1.5 us (2%)
    pallas_call x1, Pallas kernels, body(): pl.pallas_call(kernel, name='swav', out_shape=(pltpu.VMEM((B, D), F32), p...  90.9 us

profile of v5, /device:TPU:1, one launch (start us, length us, event | category | flops | bytes accessed | tf_op | source)
XLA Modules:
  0.0 95.3 jit_solution(13128725111569501038)
XLA Ops:
  1.3 90.9 %swav.1 = (f32[256,256]{1,0:T(8,128)S(1)}, f32[16,8192]{1,0:T(8,128)S(1)}, f32[1]{0:T(128)}) custom-call(s32[1]{0:T(128)S(6)} %copy.13.fill_ref, bf16[256,256]{1,0:T(8,128)(2,1)} %emb_hbm.1, bf16[512,256]{1,0:T(8,128)(2,1)} %queue_hbm.1, bf16[16,8192]{1,0:T(8,128)(2,1)} %proto_hbm.1, s32[1,256]{1,0:T(1,128)} %bitcast.1), custom_call_target="tpu_custom_call" | custom-call | tf_op jit(solution)/shard_map/swav/pallas_call | solution.py:617
  92.1 0.7 copy.11
  92.9 0.8 copy.12

commit v6 on v5

--- a/solution.py
+++ b/solution.py
@@ -57,7 +57,7 @@
     emb_ref, queue_ref, proto_ref, rows, protos, massf, massb, row_acc, row_wide, score, grad, turned, soft_acc, col_acc, alive, row16, col16, colb,
     col_part, row_part, row_mid, col_in, rowx_in, rowy_in,
     row_soft, row_code, unit, factor, back,
-    gp_out, gp_in, ng_out, ngc_in, ng_pair, ng_in, ng_sum, ngy_in, ng_all, lx_in, lz_in,
+    upright, gp_out, gp_in, ng_out, ngc_in, ng_pair, ng_in, ng_sum, ngy_in, ng_all, lx_in, lz_in,
     a_send, a_recv, z_send, z_recv, r_send, r_recv, f_send, f_recv,
     c_send, c_recv, x_send, x_recv, y_send, y_recv,
     g_send, g_recv, e_send, e_recv, n_send, n_recv, m_send, m_recv, h_send, h_recv, lx_send, lx_recv, lz_send, lz_recv, in_sem,
@@ -247,12 +247,38 @@
     for j in range(tiles):
         col_part[0, j:j + 1, :] = jnp.sum(col_acc[:, j * TILE:(j + 1) * TILE], axis=0, keepdims=True)
 
+    def idle_work(t):
+        eye = jnp.where(rid == cid, 1.0, 0.0).astype(BF16)
+        if t == 0:
+            for slot in range(SIDE):
+                turned[:, slot * B:(slot + 1) * B] = lax.dot_general(
+                    eye, rows[slot, 0:B, :], NT, preferred_element_type=F32
+                ).astype(BF16)
+                row_part[last, 2 * slot + 1:2 * slot + 2, 0:B] = jnp.concatenate(
+                    [
+                        jnp.sum(soft_acc[slot, 0:128, :].T, axis=0, keepdims=True),
+                        jnp.sum(soft_acc[slot, 128:256, :].T, axis=0, keepdims=True),
+                    ],
+                    axis=1,
+                )
+                row_part[last, 2 * slot:2 * slot + 2, B:half] = jnp.ones((2, half - B), F32)
+        elif t == 1:
+            for j in range(tiles):
+                at = slice(j * TILE, (j + 1) * TILE)
+                upright[at, :] = lax.dot_general(
+                    eye, protos[:, at], NT, preferred_element_type=F32
+                ).astype(BF16)
+
+    last = ITERS - 1
+    half = R // 2
+
     def column_exchange(t):
         for d in (2, 1, 3):
             remote(
                 col_part.at[t], col_in.at[t, z], c_send, c_recv.at[t], (z_peer(d) * SIDE + y, me)
             )
         col_in[t, z] = col_part[t]
+        idle_work(t)
         landed(col_in.at[t, 0:SIDE - 1], c_recv.at[t])
         column = 1.0 / (col_in[t, 0] + col_in[t, 1] + col_in[t, 2] + col_in[t, 3])
         for j in range(tiles):
@@ -302,7 +328,6 @@
     def turn(slot, b):
         return jnp.sum(row_acc[slot, b * 128:(b + 1) * 128, :].T, axis=0, keepdims=True)
 
-    half = R // 2
     rid8, lane8 = iota((8, half), 0), iota((8, half), 1)
     spot = lax.rem(rid8, 2) * half + lane8
     queue_row = (z * SIDE + rid8 // 2) * Q + spot - B
@@ -348,23 +373,10 @@
             at = slice((n % 2) * 128, (n % 2 + 1) * 128)
             col_part[t + 1, n // 2:n // 2 + 1, at] = jnp.sum(sums[n], axis=0, keepdims=True)
 
-    last = ITERS - 1
     for slot in range(SIDE):
         row_sums(slot, B)
         for b in range(B // 128):
             row_part[last, 2 * slot:2 * slot + 1, b * 128:(b + 1) * 128] = turn(slot, b)
-        row_part[last, 2 * slot + 1:2 * slot + 2, 0:B] = jnp.concatenate(
-            [
-                jnp.sum(soft_acc[slot, 0:128, :].T, axis=0, keepdims=True),
-                jnp.sum(soft_acc[slot, 128:256, :].T, axis=0, keepdims=True),
-            ],
-            axis=1,
-        )
-        row_part[last, 2 * slot:2 * slot + 2, B:half] = jnp.ones((2, half - B), F32)
-        eye = jnp.where(rid == cid, 1.0, 0.0).astype(BF16)
-        turned[:, slot * B:(slot + 1) * B] = lax.dot_general(
-            eye, rows[slot, 0:B, :], NT, preferred_element_type=F32
-        ).astype(BF16)
     sums = row_exchange(last)
     for slot in range(SIDE):
         code = sums[2 * slot:2 * slot + 1, 0:B]
@@ -406,10 +418,6 @@
                     grad[slot, at, lanes] = (softs[c] - goal).astype(BF16)
         return lost
 
-    def normed_chunk(slot, k):
-        cols = pl.ds(pl.multiple_of(k * span, span), span)
-        return lax.dot_general(grad[slot, :, cols], protos[:, cols], NT, preferred_element_type=F32)
-
     side = B // 2
     own_half = pl.ds(pl.multiple_of(core * side, side), side)
     other_half = pl.ds(pl.multiple_of((1 - core) * side, side), side)
@@ -432,7 +440,7 @@
         landed(ng_in.at[n, 0:SIDE - 1], n_recv.at[n])
         return ng_in[n, 0] + ng_in[n, 1] + ng_in[n, 2] + ng_in[n, 3]
 
-    def send_protos(k):
+    def make_protos(k):
         for h in range(span // TILE):
             cols = slice(k * span + h * TILE, k * span + (h + 1) * TILE)
             part = jnp.dot(turned[:, 0:B], grad[0, :, cols], preferred_element_type=F32)
@@ -442,6 +450,8 @@
                     preferred_element_type=F32,
                 )
             gp_out[:, cols] = part.astype(BF16)
+
+    def send_protos(k):
         for dz, dy in (
             (2, 2), (2, 1), (2, 3), (1, 2), (3, 2), (1, 1), (1, 3), (3, 1), (3, 3),
             (2, 0), (0, 2), (1, 0), (3, 0), (0, 1), (0, 3),
@@ -459,34 +469,25 @@
 
     order = (2, 1, 3, 0)
     lost = jnp.zeros((8, 128), F32)
-    for n in range(SIDE):
-        slot = y_peer(order[n])
-        if n:
-            ng_out[n - 1] = jnp.zeros((B, D), F32)
-
-        def block_chunk(k, lost, n=n, slot=slot):
-            lost = slope_chunk(slot, k, lost)
-            if n:
-                ng_out[n - 1] += normed_chunk(y_peer(order[n - 1]), k)
-            return lost
-
-        lost = lax.fori_loop(0, chunks, block_chunk, lost)
-        if n >= 1:
-            to_sibling(n - 1)
-        if n >= 2:
-            to_chips(n - 2)
+    for k in range(chunks):
+        lost = lax.fori_loop(0, SIDE, lambda slot, lost, k=k: slope_chunk(slot, k, lost), lost)
+        if k + 1 < chunks:
+            make_protos(k)
+            send_protos(k)
     lx_in[me] = logs - lost * (math.log(2.0) / 10.0)
     for d in range(1, LANES):
         remote(lx_in.at[me], lx_in.at[me], lx_send, lx_recv, (row, p_peer(d)))
-    ng_out[SIDE - 1] = lax.dot_general(grad[y], protos[...], NT, preferred_element_type=F32)
-    to_sibling(SIDE - 1)
-    to_chips(SIDE - 2)
-    send_protos(0)
+    for n in range(SIDE):
+        ng_out[n] = jnp.dot(grad[y_peer(order[n])], upright[...], preferred_element_type=F32)
+        to_sibling(n)
+        if n:
+            to_chips(n - 1)
+    make_protos(chunks - 1)
     to_chips(SIDE - 1)
-    send_protos(1)
     pass_normed(0)
     pass_normed(1)
     pass_normed(2)
+    send_protos(chunks - 1)
     landed(lx_in.at[0:LANES - 1], lx_recv)
     lost = lx_in[0]
     for k in range(1, LANES):
@@ -498,8 +499,6 @@
                 remote(
                     lz_in.at[row], lz_in.at[row], lz_send, lz_recv, (z_peer(dz) * SIDE + y_peer(dy), me)
                 )
-    send_protos(2)
-    send_protos(3)
     total = sum_normed(3)
     landed(ngy_in.at[0:SIDE - 1], m_recv)
     mine_at = core * SIDE + chip
@@ -599,6 +598,7 @@
         pltpu.VMEM((B, D), F32),
         pltpu.VMEM((B, 128), F32),
         pltpu.VMEM((B, B), BF16),
+        pltpu.VMEM((width, D), BF16),
         pltpu.VMEM((D, width), BF16),
         pltpu.VMEM((SIDE, SIDE, chunks, 16, width // chunks), BF16),
         pltpu.VMEM((SIDE, B, D), F32),

time: 95.5 us -> 93.1 us (0.975)
  Pallas kernels: 90.9 us -> 88.5 us
    pallas_call x1, Pallas kernels: 90.9 us -> 88.5 us  [body(): pl.pallas_call(kernel, name='swav', out_shape=(pltpu.VMEM((B, D), F32), p...]
where the time goes in v6:
time: 93.1 us; the launch traced here: 92.9 us
  Pallas kernels  88.5 us (95%)
  between operations  2.98 us (3%)
  local copies, waits for them, and re-layouts  1.5 us (2%)
    pallas_call x1, Pallas kernels, body(): pl.pallas_call(kernel, name='swav', out_shape=(pltpu.VMEM((B, D), F32), p...  88.5 us

profile of v6, /device:TPU:1, one launch (start us, length us, event | category | flops | bytes accessed | tf_op | source)
XLA Modules:
  0.0 92.9 jit_solution(4107879101381015435)
XLA Ops:
  1.3 88.5 %swav.1 = (f32[256,256]{1,0:T(8,128)S(1)}, f32[16,8192]{1,0:T(8,128)S(1)}, f32[1]{0:T(128)}) custom-call(s32[1]{0:T(128)S(6)} %copy.13.fill_ref, bf16[256,256]{1,0:T(8,128)(2,1)} %emb_hbm.1, bf16[512,256]{1,0:T(8,128)(2,1)} %queue_hbm.1, bf16[16,8192]{1,0:T(8,128)(2,1)} %proto_hbm.1, s32[1,256]{1,0:T(1,128)} %bitcast.1), custom_call_target="tpu_custom_call" | custom-call | tf_op jit(solution)/shard_map/swav/pallas_call | solution.py:617
  89.7 0.7 copy.11
  90.4 0.8 copy.12

commit v7 on v6

--- a/solution.py
+++ b/solution.py
@@ -21,7 +21,7 @@
 B = 256
 Q = 512
 R = B + Q
-V = 512
+V = 384
 D = 256
 TILE = 256
 NT = (((1,), (1,)), ((), ()))
@@ -52,9 +52,9 @@
 
 
 def kernel(
-    fill_ref, emb_hbm, queue_hbm, proto_hbm, image_ref,
+    fill_ref, emb_hbm, queue_hbm, proto_hbm, image_hbm,
     ge_ref, gp_ref, loss_ref,
-    emb_ref, queue_ref, proto_ref, rows, protos, massf, massb, row_acc, row_wide, score, grad, turned, soft_acc, col_acc, alive, row16, col16, colb,
+    emb_ref, queue_ref, proto_ref, image_ref, rows, protos, massf, massb, row_acc, row_wide, score, grad, turned, soft_acc, col_acc, alive, row16, col16, colb,
     col_part, row_part, row_mid, col_in, rowx_in, rowy_in,
     row_soft, row_code, unit, factor, back,
     upright, gp_out, gp_in, ng_out, ngc_in, ng_pair, ng_in, ng_sum, ngy_in, ng_all, lx_in, lz_in,
@@ -105,7 +105,7 @@
 
     loads = []
     for n, (source, target) in enumerate(
-        ((emb_hbm, emb_ref), (queue_hbm, queue_ref), (proto_hbm, proto_ref))
+        ((image_hbm, image_ref), (emb_hbm, emb_ref), (queue_hbm, queue_ref), (proto_hbm, proto_ref))
     ):
         loads.append(pltpu.make_async_copy(source, target, in_sem.at[n]))
         loads[-1].start()
@@ -119,6 +119,8 @@
         pl.semaphore_signal(barrier, inc=1, device_id=(row, p_peer(d)), device_id_type=MESH)
         count += 1
 
+    for copy in loads:
+        copy.wait()
     image = image_ref[...].astype(F32)
     wide = jnp.broadcast_to(image, (B, B))
     rid, cid = iota((B, B), 0), iota((B, B), 1)
@@ -127,8 +129,6 @@
     base = (row * (B // CROPS)).astype(F32)
     place = jnp.sum(jnp.where(rid < cid, same, 0.0), axis=0, keepdims=True) * (B // CROPS) + (image - base)
     forward = jnp.where(rid.astype(F32) == place, 1.0, 0.0).astype(BF16)
-    for copy in loads:
-        copy.wait()
     exact, _ = unit_rows(emb_ref[...])
     ordered = jnp.dot(forward, exact.astype(BF16), preferred_element_type=F32).astype(BF16)
     rows[y, 0:B, :] = ordered
@@ -342,7 +342,8 @@
             row_sums(slot, V)
             rest = lax.dot_general(col16[...], massb[slot], NT, preferred_element_type=F32)
             rest = jnp.sum(rest, axis=0, keepdims=True)
-            parts = [turn(slot, b) for b in range(V // 128)] + [rest[:, 0:128], rest[:, 128:256]]
+            parts = [turn(slot, b) for b in range(V // 128)]
+            parts += [rest[:, b * 128:(b + 1) * 128] for b in range((R - V) // 128)]
             for h in range(2):
                 row_part[t, pl.ds(2 * slot + h, 1), :] = jnp.concatenate(parts[3 * h:3 * h + 3], axis=1)
             return carry
@@ -350,7 +351,7 @@
         lax.fori_loop(0, SIDE, row_block, 0)
         weight = live / row_exchange(t)
         for slot in range(SIDE):
-            row16[slot] = stack16(weight[2 * slot + 1:2 * slot + 2, 128:half])
+            row16[slot] = stack16(weight[2 * slot + 1:2 * slot + 2, V - half:half])
             for b in range(V // 128):
                 at = slice((b % 3) * 128, (b % 3 + 1) * 128)
                 line = weight[2 * slot + b // 3:2 * slot + b // 3 + 1, at]
@@ -471,7 +472,7 @@
     lost = jnp.zeros((8, 128), F32)
     for k in range(chunks):
         lost = lax.fori_loop(0, SIDE, lambda slot, lost, k=k: slope_chunk(slot, k, lost), lost)
-        if k + 1 < chunks:
+        if k + 2 < chunks:
             make_protos(k)
             send_protos(k)
     lx_in[me] = logs - lost * (math.log(2.0) / 10.0)
@@ -482,6 +483,9 @@
         to_sibling(n)
         if n:
             to_chips(n - 1)
+        if n == 1:
+            make_protos(chunks - 2)
+            send_protos(chunks - 2)
     make_protos(chunks - 1)
     to_chips(SIDE - 1)
     pass_normed(0)
@@ -572,6 +576,7 @@
         pltpu.VMEM((B, D), BF16),
         pltpu.VMEM((Q, D), BF16),
         pltpu.VMEM(prototypes.shape, BF16),
+        pltpu.VMEM((1, B), jnp.int32),
         pltpu.VMEM((SIDE, R, D), BF16),
         pltpu.VMEM((D, width), BF16),
         pltpu.VMEM((SIDE, V, width), F32),
@@ -612,7 +617,7 @@
         pltpu.VMEM((SIDE * SIDE, 8, 128), F32),
         *group(chunks, SIDE), *group(chunks), *group(SIDE), *group(SIDE),
         *group(ITERS), *group(ITERS), *group(ITERS),
-        *group(), *group(SIDE), *group(SIDE), *group(), *group(), *group(), *group(), dma((3,)),
+        *group(), *group(SIDE), *group(SIDE), *group(), *group(), *group(), *group(), dma((4,)),
     ]
     return pl.pallas_call(
         kernel,
@@ -622,7 +627,7 @@
             pltpu.VMEM((prototypes.shape[0], prototypes.shape[1]), F32),
             jax.ShapeDtypeStruct((1,), F32),
         ),
-        in_specs=[smem, hbm, hbm, hbm, vmem],
+        in_specs=[smem, hbm, hbm, hbm, hbm],
         out_specs=(vmem, vmem, smem),
         scratch_shapes=scratch,
         compiler_params=pltpu.CompilerParams(

time: 93.1 us -> 92.7 us (level)
  no operation moved by 1% of the time
where the time goes in v7:
time: 92.7 us; the launch traced here: 92.6 us
  Pallas kernels  88.1 us (95%)
  between operations  2.98 us (3%)
  local copies, waits for them, and re-layouts  1.5 us (2%)
    pallas_call x1, Pallas kernels, body(): pl.pallas_call(kernel, name='swav', out_shape=(pltpu.VMEM((B, D), F32), p...  88.1 us

profile of v7, /device:TPU:1, one launch (start us, length us, event | category | flops | bytes accessed | tf_op | source)
XLA Modules:
  0.0 92.6 jit_solution(6662287638266215620)
XLA Ops:
  1.3 88.1 %swav.1 = (f32[256,256]{1,0:T(8,128)S(1)}, f32[16,8192]{1,0:T(8,128)S(1)}, f32[1]{0:T(128)}) custom-call(s32[1]{0:T(128)S(6)} %copy.13.fill_ref, bf16[256,256]{1,0:T(8,128)(2,1)} %emb_hbm.1, bf16[512,256]{1,0:T(8,128)(2,1)} %queue_hbm.1, bf16[16,8192]{1,0:T(8,128)(2,1)} %proto_hbm.1, s32[1,256]{1,0:T(1,128)} %bitcast.1), custom_call_target="tpu_custom_call" | custom-call | tf_op jit(solution)/shard_map/swav/pallas_call | solution.py:622
  89.4 0.7 copy.11
  90.1 0.8 copy.12

commit v8 on v7

--- a/solution.py
+++ b/solution.py
@@ -625,7 +625,7 @@
         out_shape=(
             pltpu.VMEM((B, D), F32),
             pltpu.VMEM((prototypes.shape[0], prototypes.shape[1]), F32),
-            jax.ShapeDtypeStruct((1,), F32),
+            pltpu.SMEM((1,), F32),
         ),
         in_specs=[smem, hbm, hbm, hbm, hbm],
         out_specs=(vmem, vmem, smem),

time: 92.7 us -> 91 us (0.982)
  between operations: 2.98 us -> 1.81 us
where the time goes in v8:
time: 91 us; the launch traced here: 90.9 us
  Pallas kernels  87.6 us (96%)
  between operations  1.81 us (2%)
  local copies, waits for them, and re-layouts  1.5 us (2%)
    pallas_call x1, Pallas kernels, body(): pl.pallas_call(kernel, name='swav', out_shape=(pltpu.VMEM((B, D), F32), p...  87.6 us

profile of v8, /device:TPU:1, one launch (start us, length us, event | category | flops | bytes accessed | tf_op | source)
XLA Modules:
  0.0 90.9 jit_solution(17724978586225790592)
XLA Ops:
  1.3 87.6 %swav.1 = (f32[256,256]{1,0:T(8,128)S(1)}, f32[16,8192]{1,0:T(8,128)S(1)}, f32[1]{0:T(128)S(4)}) custom-call(s32[1]{0:T(128)S(6)} %copy.14.fill_ref, bf16[256,256]{1,0:T(8,128)(2,1)} %emb_hbm.1, bf16[512,256]{1,0:T(8,128)(2,1)} %queue_hbm.1, bf16[16,8192]{1,0:T(8,128)(2,1)} %proto_hbm.1, s32[1,256]{1,0:T(1,128)} %bitcast.1), custom_call_target="tpu_custom_call" | custom-call | tf_op jit(solution)/shard_map/swav/pallas_call | solution.py:622
  89.4 0.7 copy.11
  90.1 0.8 copy.12
